TPU v7x, 128 devices: a whole 4x4x4 slice. The times are simulated.
128 devices in a mesh: fronts: 8 (over y, core), rows: 16 (over z, x).
Axes of the slice: x: 4, y: 4, z: 4, core: 2. Of those that a mesh axis runs over, the one named last changes fastest.
Arguments:
- lower_rhs: float32 [16, 16384, 512], P('fronts', 'rows'), may hold values from -6 to 6
- lower_vectors: float32 [16, 16384, 256], P('fronts', 'rows')
- lower_factors: float32 [16, 16, 256, 256], P('fronts', 'rows')
- merge_vectors: float32 [16, 16, 256, 256], P('fronts', 'rows')
- merge_factors: float32 [16, 16, 256, 256], P('fronts', 'rows')
- live_blocks: int32 [16], replicated, may hold values from 1 to 16, 128 in all
- parent_front: int32 [16, 1], replicated, may hold values from 0 to 7, as said below
- front_owner: int32 [8], replicated, may hold values from 0 to 7, as said below
- contrib_rows: int32 [16, 128], replicated, may hold values from 0 to 16383, as said below
- upper_rhs: float32 [8, 16384, 512], P('fronts', 'rows'), may hold values from -6 to 6
- upper_vectors: float32 [8, 16384, 256], P('fronts', 'rows')
- upper_factors: float32 [8, 16, 256, 256], P('fronts', 'rows')
- summit_vectors: float32 [8, 16, 256, 256], P('fronts', 'rows')
- summit_factors: float32 [8, 16, 256, 256], P('fronts', 'rows')
Outputs:
- lower_result: float32 [16, 16384, 512], P('fronts', 'rows')
- upper_result: float32 [8, 16384, 512], P('fronts', 'rows')
Inputs may be any that keep to these rules, and one draw needn't show every extreme that they name: `parent_front`: every parent front has between one and 4 children, and some parent has exactly 4. `front_owner`: each parent front has its own index of fronts. `contrib_rows`: row k of a child's contribution lands in its parent's row block k // 8; no two entries are equal.
All inputs are finite; a program needn't handle non-finite values.
Results may differ from a plain program's by a relative error of at most 0.0003.
Values sent between devices are 32-bit elements; how exact they have to be, the bound alone decides.
No kernel may reach another device: no remote copies, remote signals or barrier semaphores. Data moves between devices by JAX's collectives and lax.ppermute only.
A program may use at most 128 MiB of HBM per device.

v0:
```python
import jax
import jax.numpy as jnp
from jax import lax
from jax.experimental import pallas as pl
from jax.experimental.pallas import tpu as pltpu
from jax.sharding import PartitionSpec as P


N = 512
BR = 1024
K = 256
NPIV = 128
CB = 128
LEVELS = 4
F32 = jnp.float32
BF16 = jnp.bfloat16
HBM = pl.BlockSpec(memory_space=pl.ANY)


NN = ((1,), (0,))
NT = ((1,), (1,))


def split(x):
    high = x.astype(BF16)
    return high, (x - high.astype(F32)).astype(BF16)


def dot3(a, b, dims):
    def one(p, q):
        return lax.dot_general(p, q, (dims, ((), ())), preferred_element_type=F32)

    return one(a[0], b[0]) + (one(a[0], b[1]) + one(a[1], b[0]))


def full(shape):
    return pl.BlockSpec(shape, lambda *_: (0,) * len(shape))


def spec(shape, index):
    return pl.BlockSpec(shape, lambda *_: index)


def params():
    return pltpu.CompilerParams(vmem_limit_bytes=48 * 1024 * 1024)


def role(info, live_at, level):
    place = info[0]
    step = 1 << level
    at = place % (2 * step)
    live = info[live_at]
    rest = (at == step) & (place < live)
    lead = (at == 0) & (place + step < live)
    return lead, rest


def block_step(info, live_at, front, rhs, vectors, factors, prior, after=()):
    def kernel(info, x_ref, y_ref, g_ref, *rest):
        out_ref, top_ref = rest[-2:]
        active = info[0] < info[live_at]

        @pl.when(active)
        def _():
            x, y = x_ref[0], y_ref[0]
            project = dot3(split(y.T), split(x), NN)
            scaled = dot3(split(g_ref[0].T), split(project), NN)
            out_ref[0] = x - dot3(split(y), split(scaled), NN)

        @pl.when(jnp.logical_not(active))
        def _():
            out_ref[0] = x_ref[0]

        top_ref[...] = out_ref[0, :K]

    operands = [info, rhs, vectors, factors, *after] + ([] if prior is None else [prior])
    return pl.pallas_call(
        kernel,
        grid_spec=pltpu.PrefetchScalarGridSpec(
            num_scalar_prefetch=1,
            grid=(1,),
            in_specs=[
                spec((1, BR, N), (front, 0, 0)),
                spec((1, BR, K), (front, 0, 0)),
                spec((1, K, K), (front, 0, 0)),
            ]
            + [HBM] * (len(operands) - 4),
            out_specs=[spec((1, BR, N), (front, 0, 0)), full((K, N))],
        ),
        out_shape=[jax.ShapeDtypeStruct(rhs.shape, F32), jax.ShapeDtypeStruct((K, N), F32)],
        input_output_aliases={} if prior is None else {len(operands) - 1: 0},
        compiler_params=params(),
    )(*operands)


def parent_before(info, rhs, vectors, factors, node_vectors, rows, after=()):
    def kernel(info, x_ref, y_ref, g_ref, v_ref, rows_ref, *rest):
        out_ref, unit_ref, send_ref, wide = rest[-4:]
        chosen = lax.broadcasted_iota(jnp.int32, (BR, CB), 0) == rows_ref[0:1, :]
        chosen = jnp.where(chosen, 1.0, 0.0)
        taken = jnp.max(chosen, axis=1, keepdims=True) > 0.5
        wide[:, :N] = jnp.where(taken, 0.0, x_ref[0])
        wide[:, N:] = chosen
        y = y_ref[0]
        project = dot3(split(y.T), split(wide[...]), NN)
        scaled = dot3(split(g_ref[0].T), split(project), NN)
        wide[...] = wide[...] - dot3(split(y), split(scaled), NN)
        out_ref[0] = wide[:, :N]
        unit_ref[...] = wide[:, N:]

        @pl.when(info[0] % 2 == 1)
        def _():
            send_ref[...] = dot3(split(v_ref[0].T), split(wide[:K]), NN)

        @pl.when(info[0] % 2 == 0)
        def _():
            send_ref[...] = wide[:K]

    return pl.pallas_call(
        kernel,
        grid_spec=pltpu.PrefetchScalarGridSpec(
            num_scalar_prefetch=1,
            grid=(1,),
            in_specs=[full((1, BR, N)), full((1, BR, K)), full((1, K, K)), full((1, K, K)), full(rows.shape)]
            + [HBM] * len(after),
            out_specs=[full((1, BR, N)), full((BR, CB)), full((K, N + CB))],
            scratch_shapes=[pltpu.VMEM((BR, N + CB), F32)],
        ),
        out_shape=[
            jax.ShapeDtypeStruct(rhs.shape, F32),
            jax.ShapeDtypeStruct((BR, CB), F32),
            jax.ShapeDtypeStruct((K, N + CB), F32),
        ],
        compiler_params=params(),
        name="parent_before",
    )(info, rhs, vectors, factors, node_vectors, rows, *after)


def parent_after(upper, unit, send, portion, after=()):
    half = N // 2

    def kernel(x_ref, unit_ref, send_ref, data_ref, *rest):
        out_ref, send0, send1 = rest[-3:]
        data = split(data_ref[...].reshape(CB, N))
        sent = send_ref[:, :N] + dot3(split(send_ref[:, N:]), data, NN)
        send0[...] = sent[:, :half]
        send1[...] = sent[:, half:]
        out_ref[0] = x_ref[0] + dot3(split(unit_ref[...]), data, NN)

    out = jax.ShapeDtypeStruct((K, half), F32)
    return pl.pallas_call(
        kernel,
        grid=(1,),
        in_specs=[full(upper.shape), full(unit.shape), full(send.shape), full(portion.shape)] + [HBM] * len(after),
        out_specs=[full(upper.shape), full(out.shape), full(out.shape)],
        out_shape=[jax.ShapeDtypeStruct(upper.shape, F32), out, out],
        input_output_aliases={0: 0},
        compiler_params=params(),
        name="parent_after",
    )(upper, unit, send, portion, *after)


def tree_level(info, live_at, level, front, top, top_spec, send, recv, node_vectors, node_factors, lead_factors, after=()):
    cols = send.shape[1]
    last = level == LEVELS - 1

    def kernel(info, top_ref, send_ref, recv_ref, v_ref, g_ref, gl_ref, *outs):
        out_ref, *outs = outs[len(after) :]
        lead, rest = role(info, live_at, level)
        top = top_ref[...].reshape(K, cols)

        @pl.when(lead)
        def _():
            inner = send_ref[...] + recv_ref[...]
            out_ref[...] = top - dot3(split(gl_ref[0].T), split(inner), NN)

        @pl.when(rest)
        def _():
            inner = send_ref[...] + recv_ref[...]
            weight = dot3(split(g_ref[0].T), split(inner), NN)
            out_ref[...] = top - dot3(split(v_ref[0]), split(weight), NN)

        @pl.when(jnp.logical_not(lead | rest))
        def _():
            out_ref[...] = top

        if not last:
            at = info[0] % (4 << level)

            @pl.when(at == (2 << level))
            def _():
                outs[0][...] = dot3(split(v_ref[0].T), split(out_ref[...]), NN)

            @pl.when(at == 0)
            def _():
                outs[0][...] = out_ref[...]

    node = spec((1, K, K), (front, 0, 0))
    shape = jax.ShapeDtypeStruct((K, cols), F32)
    flat = full((K, cols))
    count = 1 if last else 2
    outs = pl.pallas_call(
        kernel,
        grid_spec=pltpu.PrefetchScalarGridSpec(
            num_scalar_prefetch=1,
            grid=(1,),
            in_specs=[top_spec, flat, flat, node, node, node] + [HBM] * len(after),
            out_specs=[flat] * count,
        ),
        out_shape=[shape] * count,
        compiler_params=params(),
    )(info, top, send, recv, node_vectors, node_factors, lead_factors, *after)
    return outs


def exchange(value, level):
    return lax.ppermute(value, "rows", [(i, i ^ (1 << level)) for i in range(16)])


def lead_gets(value, level):
    step = 1 << level
    return lax.ppermute(value, "rows", [(b + step, b) for b in range(0, 16, 2 * step)])


def node_level(info, live_at, level, front, applied, lead, rest, node_vectors, node_factors, after=()):
    last = level == LEVELS - 1
    height = NPIV if last else K
    rests = [] if rest is None else [rest]

    def kernel(info, _, v_ref, g_ref, lead_ref, *refs):
        out_ref, lead_out, v, g, lead, moved, kept, sems = refs[-8:]
        rows = out_ref.at[front, pl.ds(0, K)]
        step = 1 << level
        node = info[0] % (2 * step) == step
        active = info[0] < info[live_at]

        @pl.when(node)
        def _():
            ins = [
                pltpu.make_async_copy(refs[0] if rests else rows, moved, sems.at[0]),
                pltpu.make_async_copy(v_ref.at[front], v, sems.at[1]),
                pltpu.make_async_copy(lead_ref, lead, sems.at[2]),
                pltpu.make_async_copy(g_ref.at[front], g, sems.at[3]),
            ]
            for copy in ins:
                copy.start()
            for copy in ins:
                copy.wait()

            @pl.when(active)
            def _():
                inner = lead[...] + dot3(split(v[...].T), split(moved[...]), NN)
                weight = dot3(split(g[...].T), split(inner), NN)
                lead[:height] = lead[:height] - weight[:height]
                kept[...] = moved[...] - dot3(split(v[...]), split(weight), NN)

            @pl.when(jnp.logical_not(active))
            def _():
                kept[...] = moved[...]

            outs = [
                pltpu.make_async_copy(lead.at[pl.ds(0, height)], lead_out, sems.at[4]),
                pltpu.make_async_copy(kept, rows, sems.at[5]),
            ]
            for copy in outs:
                copy.start()
            for copy in outs:
                copy.wait()

        if last:

            @pl.when(info[0] == 0)
            def _():
                kept[NPIV:] = jnp.zeros((K - NPIV, N), F32)
                copy = pltpu.make_async_copy(
                    kept.at[pl.ds(NPIV, K - NPIV)], out_ref.at[front, pl.ds(NPIV, K - NPIV)], sems.at[5]
                )
                copy.start()
                copy.wait()

    square, flat = pltpu.VMEM((K, K), F32), pltpu.VMEM((K, N), F32)
    return pl.pallas_call(
        kernel,
        grid_spec=pltpu.PrefetchScalarGridSpec(
            num_scalar_prefetch=1,
            grid=(1,),
            in_specs=[HBM] * (4 + len(rests) + len(after)),
            out_specs=[HBM, HBM],
            scratch_shapes=[square, square, flat, flat, flat, pltpu.SemaphoreType.DMA((6,))],
        ),
        out_shape=[jax.ShapeDtypeStruct(applied.shape, F32), jax.ShapeDtypeStruct((height, N), F32)],
        input_output_aliases={1: 0},
        compiler_params=params(),
    )(info, applied, node_vectors, node_factors, lead, *rests, *after)


def lead_moves(value, level):
    if level == 0:
        return lax.ppermute(value, "rows", [(i, i + 1) for i in range(0, 16, 2)]), None
    step = 1 << level
    at = [(b, b + step) for b in range(0, 16, 2 * step)]
    return (
        lax.ppermute(value, "rows", [(b + step // 2, p) for b, p in at]),
        lax.ppermute(value, "rows", [(p + step // 2, p) for b, p in at]),
    )


def fill_roots(info, applied, leads):
    def kernel(info, *refs):
        out_ref, sems = refs[-2:]

        @pl.when(info[0] == 0)
        def _():
            copies = [
                pltpu.make_async_copy(refs[f], out_ref.at[f, pl.ds(0, NPIV)], sems.at[f]) for f in range(len(leads))
            ]
            for copy in copies:
                copy.start()
            for copy in copies:
                copy.wait()

    return pl.pallas_call(
        kernel,
        grid_spec=pltpu.PrefetchScalarGridSpec(
            num_scalar_prefetch=1,
            grid=(1,),
            in_specs=[HBM] * (len(leads) + 1),
            out_specs=HBM,
            scratch_shapes=[pltpu.SemaphoreType.DMA((len(leads),))],
        ),
        out_shape=jax.ShapeDtypeStruct(applied.shape, F32),
        input_output_aliases={len(leads) + 1: 0},
        compiler_params=params(),
        name="fill_roots",
    )(info, *leads, applied)


def fill_tops(info, applied, front, tops, clear):
    half = N // len(tops)

    def kernel(info, *refs):
        out_ref = refs[-1]
        for i in range(len(tops)):
            out_ref[0, :, i * half : (i + 1) * half] = refs[i][...]
        if clear:

            @pl.when(info[0] == 0)
            def _():
                out_ref[0, NPIV:, :] = jnp.zeros((K - NPIV, N), F32)

    return pl.pallas_call(
        kernel,
        grid_spec=pltpu.PrefetchScalarGridSpec(
            num_scalar_prefetch=1,
            grid=(1,),
            in_specs=[full((K, half))] * len(tops) + [HBM],
            out_specs=spec((1, K, N), (front, 0, 0)),
        ),
        out_shape=jax.ShapeDtypeStruct(applied.shape, F32),
        input_output_aliases={len(tops) + 1: 0},
        compiler_params=params(),
        name="fill_tops",
    )(info, *tops, applied)


def map_node(info, level, lead_in, rest_in, node_vectors, node_factors, after=()):
    fronts = node_vectors.shape[0]
    ins = [] if lead_in is None else [lead_in, rest_in]

    def kernel(info, *refs):
        v_ref, g_ref = refs[len(ins) :][:2]
        lead_out, rest_out = refs[-2:]
        step = 1 << level

        @pl.when(info[0] % (2 * step) == step)
        def _():
            for f in range(fronts):
                if level == LEVELS - 1:
                    row = lax.broadcasted_iota(jnp.int32, (CB, K), 0)
                    col = lax.broadcasted_iota(jnp.int32, (CB, K), 1)
                    whole = jnp.where(col == row + NPIV, 1.0, 0.0)
                else:
                    whole = refs[0][f] + refs[1][f]
                active = info[0] < info[1 + f]

                @pl.when(active)
                def _():
                    scaled = dot3(split(whole), split(g_ref[f]), NT)
                    lead_out[f] = whole - scaled
                    rest_out[f] = -dot3(split(scaled), split(v_ref[f]), NT)

                @pl.when(jnp.logical_not(active))
                def _():
                    lead_out[f] = whole
                    rest_out[f] = jnp.zeros((CB, K), F32)

    shape = jax.ShapeDtypeStruct((fronts, CB, K), F32)
    return pl.pallas_call(
        kernel,
        grid_spec=pltpu.PrefetchScalarGridSpec(
            num_scalar_prefetch=1,
            grid=(1,),
            in_specs=[full((fronts, CB, K))] * len(ins) + [full((fronts, K, K))] * 2 + [HBM] * len(after),
            out_specs=[full((fronts, CB, K))] * 2,
        ),
        out_shape=[shape, shape],
        compiler_params=params(),
    )(info, *ins, node_vectors, node_factors, *after)


def map_rows(info, lead_map, rest_map, *tops, after=()):
    fronts = len(tops)

    def kernel(info, lead_ref, rest_ref, *refs):
        top_refs, out_ref = refs[:fronts], refs[-1]
        odd = info[0] % 2 == 1
        for f in range(fronts):
            chosen = jnp.where(odd, rest_ref[f], lead_ref[f])
            product = dot3(split(chosen), split(top_refs[f][...]), NN)
            out_ref[:, f] = product.reshape(16, CB // 16, N)

    return pl.pallas_call(
        kernel,
        grid_spec=pltpu.PrefetchScalarGridSpec(
            num_scalar_prefetch=1,
            grid=(1,),
            in_specs=[full((fronts, CB, K))] * 2 + [full((K, N))] * fronts + [HBM] * len(after),
            out_specs=full((16, fronts, CB // 16, N)),
        ),
        out_shape=jax.ShapeDtypeStruct((16, fronts, CB // 16, N), F32),
        compiler_params=params(),
        name="map_rows",
    )(info, lead_map, rest_map, *tops, *after)


def per_device(
    lower_rhs,
    lower_vectors,
    lower_factors,
    merge_vectors,
    merge_factors,
    live_blocks,
    parent_front,
    front_owner,
    contrib_rows,
    upper_rhs,
    upper_vectors,
    upper_factors,
    summit_vectors,
    summit_factors,
):
    place = lax.axis_index("rows")
    column = lax.axis_index("fronts")
    blocks = lax.axis_size("rows")
    fronts = lower_rhs.shape[0]
    live = lax.dynamic_slice_in_dim(live_blocks, column * fronts, fronts)
    info = jnp.concatenate([jnp.stack([place]), live, jnp.full((1,), blocks, jnp.int32)]).astype(jnp.int32)
    lower_factors, merge_vectors, merge_factors = lower_factors[:, 0], merge_vectors[:, 0], merge_factors[:, 0]
    upper_factors, summit_vectors, summit_factors = upper_factors[:, 0], summit_vectors[:, 0], summit_factors[:, 0]

    share = CB // blocks
    parents = jnp.arange(front_owner.shape[0], dtype=jnp.int32)
    target = jnp.sum(jnp.where(parent_front == parents[None, :], front_owner[None, :], 0), axis=1)
    rows_here = lax.dynamic_slice_in_dim(contrib_rows, place * share, share, 1) - place * BR
    rows_here = jnp.where((target == column)[:, None], rows_here, -1)
    rows_here = jnp.broadcast_to(rows_here.reshape(1, -1), (8, rows_here.size))

    nodes = merge_vectors, merge_factors
    blocks_in = lower_rhs, lower_vectors, lower_factors
    lead_factors = [lead_gets(summit_factors, level) for level in range(LEVELS)]
    maps = map_node(info, 3, None, None, *nodes)
    maps = maps_move(maps, [(8, 4)], [(8, 12)])
    maps = map_node(info, 2, *maps, *nodes)
    token = maps[0]
    maps = maps_move(maps, [(4, 2), (12, 10)], [(4, 6), (12, 14)])
    applied, top_a = block_step(info, 1, 0, *blocks_in, None, [token])
    in_a = lead_moves(top_a, 0)
    maps = map_node(info, 1, *maps, *nodes, [top_a])
    token = maps[0]
    at = range(2, 16, 4)
    maps = maps_move(maps, [(i, i - 1) for i in at], [(i, i + 1) for i in at])
    applied, top_b = block_step(info, 2, 1, *blocks_in, applied, [token])
    in_b = lead_moves(top_b, 0)
    maps = map_node(info, 0, *maps, *nodes, [top_b])
    lead_map = lax.ppermute(maps[0], "rows", [(i + 1, i) for i in range(0, 16, 2)])
    applied, lead_a = node_level(info, 1, 0, 0, applied, *in_a, *nodes, [maps[1]])
    in_a = lead_moves(lead_a, 1)

    pieces = map_rows(info, lead_map, maps[1], top_a, top_b, after=[lead_a])
    swapped = lax.all_to_all(pieces, "rows", 0, 0)
    applied, lead_b = node_level(info, 2, 0, 1, applied, *in_b, *nodes, [pieces])
    upper, unit, send = parent_before(
        info, upper_rhs, upper_vectors, upper_factors, summit_vectors, rows_here, [lead_b]
    )
    applied, lead_a = node_level(info, 1, 1, 0, applied, *in_a, *nodes, [unit])
    swapped, lead_a, lead_b = lax.optimization_barrier((swapped, lead_a, lead_b))
    in_b = lead_moves(lead_b, 1)
    in_a = lead_moves(lead_a, 2)
    mine = add_all(swapped)
    portion = lax.all_gather(mine, "fronts", axis=0, tiled=True)

    upper, *sends = parent_after(upper, unit, send, portion, lead_factors)
    half = N // 2
    chunks = [[upper, spec((1, K, half), (0, 0, j)), sends[j]] for j in range(2)]
    lower_steps = list(LOWER_STEPS)
    order = sends[1]
    ins = {"a": in_a, "b": in_b}
    for level in range(LEVELS):
        recvs = [exchange(chunks[j][2], level) for j in range(2)]
        for j in range(2):
            if lower_steps:
                name, at = lower_steps.pop(0)
                f = "ab".index(name)
                applied, order = node_level(info, 1 + f, at, f, applied, *ins[name], *nodes, [order])
                if at < LEVELS - 1:
                    ins[name] = lead_moves(order, at + 1)
                else:
                    ins[name] = lax.ppermute(order, "rows", [(8, 0)])
            c = chunks[j]
            outs = tree_level(
                info, 3, level, 0, c[0], c[1], c[2], recvs[j], summit_vectors, summit_factors, lead_factors[level], [order],
            )
            order = outs[0]
            c[0], c[1] = outs[0], full((K, half))
            if level < LEVELS - 1:
                c[2] = outs[1]
    in_a, in_b = ins["a"], ins["b"]
    upper_result = fill_tops(info, upper, 0, [c[0] for c in chunks], False)
    lower_result = fill_roots(info, applied, [in_a, in_b])
    return (lower_result, upper_result)


def maps_move(maps, lead_pairs, rest_pairs):
    return lax.ppermute(maps[0], "rows", lead_pairs), lax.ppermute(maps[1], "rows", rest_pairs)


def add_all(pieces):
    def kernel(in_ref, out_ref):
        total = in_ref[0]
        for i in range(1, in_ref.shape[0]):
            total = total + in_ref[i]
        out_ref[...] = total

    return pl.pallas_call(kernel, out_shape=jax.ShapeDtypeStruct(pieces.shape[1:], F32), name="add_all")(pieces)


LOWER_STEPS = (("b", 1), ("a", 2), ("b", 2), ("a", 3), ("b", 3))


def solution(mesh):
    placed = (
        P("fronts", "rows", None),
        P("fronts", "rows", None),
        P("fronts", "rows", None, None),
        P("fronts", "rows", None, None),
        P("fronts", "rows", None, None),
        P(),
        P(),
        P(),
        P(),
        P("fronts", "rows", None),
        P("fronts", "rows", None),
        P("fronts", "rows", None, None),
        P("fronts", "rows", None, None),
        P("fronts", "rows", None, None),
    )
    return jax.shard_map(
        lambda *args: per_device(*args),
        mesh=mesh,
        in_specs=placed,
        out_specs=(P("fronts", "rows", None), P("fronts", "rows", None)),
        check_vma=False,
    )
```

profile of v0, /device:TPU:0, one launch (start us, length us, event | category | flops | bytes accessed | tf_op | source)
XLA Modules:
  0.0 185.2 jit_solution(9061561374400432271)
XLA Ops:
  0.6 0.7 dynamic_slice.6
  1.4 1.0 copy-done
  2.5 1.0 copy-done.2
  4.8 0.8 collective-permute-start.1
  7.6 1.6 copy-done.7
  9.2 1.0 copy-done.9
  10.2 6.1 %shard_map.151 = (f32[2,1024,512]{2,1,0:T(8,128)}, f32[256,512]{1,0:T(8,128)S(1)}) custom-call(s32[4]{0:T(128)S(1)} %pad_add_fusion.info, f32[2,1024,512]{2,1,0:T(8,128)} %x_ref.4, f32[2,1024,256]{2,1,0:T(8,128)S(1)} %copy-done.7, f32[2,256,256]{2,1,0:T(8,128)S(1)} %bitcast.53, f32[2,128,256]{2,1,0:T(8,128)S(1)} %get-tuple-element.53.rest_0_), custom_call_target="tpu_custom_call" | custom-call | tf_op jit(solution)/shard_map/pallas_call | solution.py:77
  16.3 3.5 %collective-permute-start.4 = (f32[256,512]{1,0:T(8,128)S(1)}, f32[256,512]{1,0:T(8,128)S(1)}, u32[]{:S(2)}, u32[]{:S(2)}) collective-permute-start(f32[256,512]{1,0:T(8,128)S(1)} %get-tuple-element.55.refs_4_.refs_0_), channel_id=1, source_target_pairs={{0,1},{2,3},{4,5},{6,7},{8,9},{10,11},{12,13},{14,15},{16,17},{18,... | collective-permute-start | bytes 1572872 | tf_op jit(solution)/shard_map/ppermute | solution.py:299
  21.8 5.8 %shard_map.153 = (f32[2,1024,512]{2,1,0:T(8,128)}, f32[256,512]{1,0:T(8,128)S(1)}) custom-call(s32[4]{0:T(128)S(1)} %pad_add_fusion.info, f32[2,1024,512]{2,1,0:T(8,128)} %x_ref.4, f32[2,1024,256]{2,1,0:T(8,128)S(1)} %copy-done.8, f32[2,256,256]{2,1,0:T(8,128)S(1)} %bitcast.54, ...), custom_call_target="tpu_custom_call", output_to_operand_aliasing={{0}: (5, {})} | custom-call | tf_op jit(solution)/shard_map/pallas_call | solution.py:77
  28.2 1.3 collective-permute-start.8
  29.5 12.3 %collective-permute-start.7 = (f32[256,512]{1,0:T(8,128)S(1)}, f32[256,512]{1,0:T(8,128)S(1)}, u32[]{:S(2)}, u32[]{:S(2)}) collective-permute-start(f32[256,512]{1,0:T(8,128)S(1)} %get-tuple-element.60.refs_4_.refs_1_), channel_id=1, source_target_pairs={{0,1},{2,3},{4,5},{6,7},{8,9},{10,11},{12,13},{14,15},{16,17},{18,... | collective-permute-start | bytes 1572872 | tf_op jit(solution)/shard_map/ppermute | solution.py:299
  41.8 1.3 collective-permute-start.13
  43.1 1.3 collective-permute-start.14
  45.1 1.5 collective-permute-start.10
  46.5 1.4 collective-permute-start.9
  48.0 1.8 map_rows.1.refs_0_
  49.8 15.6 %all-to-all-start = ((f32[16,2,8,512]{3,2,1,0:T(8,128)}), f32[16,2,8,512]{3,2,1,0:T(8,128)}, u32[]{:S(2)}, u32[]{:S(2)}) async-start(f32[16,2,8,512]{3,2,1,0:T(8,128)} %map_rows.1.refs_0_), calls=%async_computation | async-start | bytes 1048576 | tf_op jit(solution)/shard_map/all_to_all | solution.py:490
  65.5 1.3 collective-permute-start.15
  67.0 0.8 shard_map.156
  67.9 0.7 copy-done.11
  69.0 5.4 %parent_before.1 = (f32[1,1024,512]{2,1,0:T(8,128)}, f32[1024,128]{1,0:T(8,128)S(1)}, f32[256,640]{1,0:T(8,128)S(1)}) custom-call(s32[4]{0:T(128)S(1)} %pad_add_fusion.info, f32[1,1024,512]{2,1,0:T(8,128)S(1)} %copy-done.11, f32[1,1024,256]{2,1,0:T(8,128)S(1)} %copy-done.12, f32[1,256,256]{2,1,0:T(8,128)S(1)} %bitcast.55, f32[1,256,256]{2,1,0:T(8,128)S(1)} %bitcast.32, ...), custom_call_target="tpu_custom_call" | custom-call | tf_op jit(solution)/shard_map/parent_before/pallas_call | solution.py:119
  74.5 0.9 copy-done.13
  76.0 0.8 copy-done.17
  76.8 1.4 collective-permute-start.11
  78.2 1.4 collective-permute-start.12
  79.7 1.3 collective-permute-start.16
  80.9 1.7 add_all.1
  84.0 13.1 %all_gather.3.data_ref = f32[16,8,512]{2,1,0:T(8,128)S(1)} all-gather(f32[2,8,512]{2,1,0:T(8,128)} %add_all.1), channel_id=1, replica_groups=mesh['fronts'=8,'rows'=16] {'fronts'}, dimensions={0}, use_global_device_ids=true | all-gather | bytes 294912 | tf_op jit(solution)/shard_map/all_gather | solution.py:500
  97.1 1.1 copy-done.14
  98.2 4.1 %parent_after.1 = (f32[1,1024,512]{2,1,0:T(8,128)}, f32[256,256]{1,0:T(8,128)S(1)}, f32[256,256]{1,0:T(8,128)S(1)}) custom-call(f32[1,1024,512]{2,1,0:T(8,128)} %get-tuple-element.71.x_ref, f32[1024,128]{1,0:T(8,128)S(1)} %get-tuple-element.67.refs_1_.unit_ref, f32[256,640]{1,0:T(8,128)S(1)} %copy-done.14, ...), custom_call_target="tpu_custom_call", output_to_operand_aliasing={{0}: (0, {})} | custom-call | tf_op jit(solution)/shard_map/parent_after/pallas_call | solution.py:151
  102.3 6.5 %collective-permute-start.19 = (f32[256,256]{1,0:T(8,128)S(1)}, f32[256,256]{1,0:T(8,128)S(1)}, u32[]{:S(2)}, u32[]{:S(2)}) collective-permute-start(f32[256,256]{1,0:T(8,128)S(1)} %get-tuple-element.78.send_ref), channel_id=1, source_target_pairs={{0,1},{1,0},{2,3},{3,2},{4,5},{5,4},{6,7},{7,6},{8,9},{9,8},{10,11... | collective-permute-start | bytes 786440 | tf_op jit(solution)/shard_map/ppermute | solution.py:217
  109.4 0.7 collective-permute-start.20
  110.8 4.8 %collective-permute-done.19.recv_ref = f32[256,256]{1,0:T(8,128)S(1)} collective-permute-done((f32[256,256]{1,0:T(8,128)S(1)}, f32[256,256]{1,0:T(8,128)S(1)}, u32[]{:S(2)}, u32[]{:S(2)}) %collective-permute-start.19) | collective-permute-done | bytes 262176 | tf_op jit(solution)/shard_map/ppermute | solution.py:217
  115.6 1.7 collective-permute-start.22
  117.3 0.9 shard_map.159
  118.9 0.7 collective-permute-start.23
  119.6 0.7 collective-permute-start.24
  120.3 3.3 %collective-permute-done.22.recv_ref = f32[256,256]{1,0:T(8,128)S(1)} collective-permute-done((f32[256,256]{1,0:T(8,128)S(1)}, f32[256,256]{1,0:T(8,128)S(1)}, u32[]{:S(2)}, u32[]{:S(2)}) %collective-permute-start.22) | collective-permute-done | bytes 262176 | tf_op jit(solution)/shard_map/ppermute | solution.py:217
  123.5 10.1 %collective-permute-start.25 = (f32[256,256]{1,0:T(8,128)S(1)}, f32[256,256]{1,0:T(8,128)S(1)}, u32[]{:S(2)}, u32[]{:S(2)}) collective-permute-start(f32[256,256]{1,0:T(8,128)S(1)} %get-tuple-element.85.send_ref), channel_id=1, source_target_pairs={{0,2},{1,3},{2,0},{3,1},{4,6},{5,7},{6,4},{7,5},{8,10},{9,11},{10,... | collective-permute-start | bytes 786440 | tf_op jit(solution)/shard_map/ppermute | solution.py:217
  133.6 0.9 shard_map.161
  134.5 0.8 shard_map.162
  135.4 0.7 collective-permute-start.27
  136.8 2.9 %collective-permute-done.25.recv_ref = f32[256,256]{1,0:T(8,128)S(1)} collective-permute-done((f32[256,256]{1,0:T(8,128)S(1)}, f32[256,256]{1,0:T(8,128)S(1)}, u32[]{:S(2)}, u32[]{:S(2)}) %collective-permute-start.25) | collective-permute-done | bytes 262176 | tf_op jit(solution)/shard_map/ppermute | solution.py:217
  139.7 3.2 %collective-permute-start.29 = (f32[256,256]{1,0:T(8,128)S(1)}, f32[256,256]{1,0:T(8,128)S(1)}, u32[]{:S(2)}, u32[]{:S(2)}) collective-permute-start(f32[256,256]{1,0:T(8,128)S(1)} %get-tuple-element.90.send_ref), channel_id=1, source_target_pairs={{0,2},{1,3},{2,0},{3,1},{4,6},{5,7},{6,4},{7,5},{8,10},{9,11},{10,... | collective-permute-start | bytes 786440 | tf_op jit(solution)/shard_map/ppermute | solution.py:217
  142.9 0.9 shard_map.163
  143.8 1.6 collective-permute-start.31
  145.4 1.3 shard_map.164
  146.8 1.7 collective-permute-done.29.recv_ref
  148.4 0.9 shard_map.165
  149.3 1.6 collective-permute-start.33
  150.9 1.3 shard_map.166
  152.3 0.9 shard_map.167
  153.2 9.3 %collective-permute-start.32 = (f32[256,256]{1,0:T(8,128)S(1)}, f32[256,256]{1,0:T(8,128)S(1)}, u32[]{:S(2)}, u32[]{:S(2)}) collective-permute-start(f32[256,256]{1,0:T(8,128)S(1)} %get-tuple-element.96.send_ref), channel_id=1, source_target_pairs={{0,8},{1,9},{2,10},{3,11},{4,12},{5,13},{6,14},{7,15},{8,0},{9,1},... | collective-permute-start | bytes 786440 | tf_op jit(solution)/shard_map/ppermute | solution.py:217
  162.5 0.9 shard_map.168
  163.4 4.7 %collective-permute-start.34 = (f32[256,256]{1,0:T(8,128)S(1)}, f32[256,256]{1,0:T(8,128)S(1)}, u32[]{:S(2)}, u32[]{:S(2)}) collective-permute-start(f32[256,256]{1,0:T(8,128)S(1)} %get-tuple-element.99.send_ref), channel_id=1, source_target_pairs={{0,8},{1,9},{2,10},{3,11},{4,12},{5,13},{6,14},{7,15},{8,0},{9,1},... | collective-permute-start | bytes 786440 | tf_op jit(solution)/shard_map/ppermute | solution.py:217
  168.1 1.3 collective-permute-start.26
  169.4 1.3 collective-permute-start.30
  170.7 0.9 shard_map.169.outs_0_.refs_0_
  171.6 3.1 %collective-permute-done.34.recv_ref = f32[256,256]{1,0:T(8,128)S(1)} collective-permute-done((f32[256,256]{1,0:T(8,128)S(1)}, f32[256,256]{1,0:T(8,128)S(1)}, u32[]{:S(2)}, u32[]{:S(2)}) %collective-permute-start.34) | collective-permute-done | bytes 262176 | tf_op jit(solution)/shard_map/ppermute | solution.py:217
  174.7 0.9 shard_map.170.refs_1_
  175.6 1.4 fill_tops.1
  177.0 3.7 %collective-permute-done.26.refs_0_ = f32[128,512]{1,0:T(8,128)S(1)} collective-permute-done((f32[128,512]{1,0:T(8,128)S(1)}, f32[128,512]{1,0:T(8,128)S(1)}, u32[]{:S(2)}, u32[]{:S(2)}) %collective-permute-start.26) | collective-permute-done | bytes 262176 | tf_op jit(solution)/shard_map/ppermute | solution.py:518
  180.7 3.0 %collective-permute-done.30.refs_1_ = f32[128,512]{1,0:T(8,128)S(1)} collective-permute-done((f32[128,512]{1,0:T(8,128)S(1)}, f32[128,512]{1,0:T(8,128)S(1)}, u32[]{:S(2)}, u32[]{:S(2)}) %collective-permute-start.30) | collective-permute-done | bytes 262176 | tf_op jit(solution)/shard_map/ppermute | solution.py:518
  183.7 1.3 fill_roots.1
  (86 shorter events, 11.8 us)
Async XLA Ops:
  1.4 1.0 copy-start
  2.5 1.0 copy-start.2
  4.1 1.5 collective-permute-start
  4.8 15.0 %copy-start.1 = (f32[2,1,256,256]{3,2,1,0:T(8,128)S(1)}, f32[2,1,256,256]{3,2,1,0:T(8,128)}, u32[]{:S(2)}) copy-start(f32[2,1,256,256]{3,2,1,0:T(8,128)} %param.17) | copy-start | bytes 1572868
  4.8 15.0 %copy-start.3 = (f32[2,1,256,256]{3,2,1,0:T(8,128)S(1)}, f32[2,1,256,256]{3,2,1,0:T(8,128)}, u32[]{:S(2)}) copy-start(f32[2,1,256,256]{3,2,1,0:T(8,128)} %param.18) | copy-start | bytes 1572868
  4.8 0.8 collective-permute-start.1
  6.2 13.6 %collective-permute-start.2 = (f32[2,128,256]{2,1,0:T(8,128)S(1)}, f32[2,128,256]{2,1,0:T(8,128)S(1)}, u32[]{:S(2)}, u32[]{:S(2)}) collective-permute-start(f32[2,128,256]{2,1,0:T(8,128)S(1)} %get-tuple-element.53.rest_0_), channel_id=1, source_target_pairs={{4,2},{12,10},{20,18},{28,26},{36,34},{44,42},{52,50},{60,58},{68,... | collective-permute-start | bytes 786440 | tf_op jit(solution)/shard_map/ppermute | solution.py:534
  6.9 12.9 %collective-permute-start.3 = (f32[2,128,256]{2,1,0:T(8,128)S(1)}, f32[2,128,256]{2,1,0:T(8,128)S(1)}, u32[]{:S(2)}, u32[]{:S(2)}) collective-permute-start(f32[2,128,256]{2,1,0:T(8,128)S(1)} %get-tuple-element.54), channel_id=1, source_target_pairs={{4,6},{12,14},{20,22},{28,30},{36,38},{44,46},{52,54},{60,62},{68,... | collective-permute-start | bytes 786440 | tf_op jit(solution)/shard_map/ppermute | solution.py:534
  7.6 1.6 copy-start.7
  9.2 1.0 copy-start.9
  10.2 11.6 %copy-start.8 = (f32[2,1024,256]{2,1,0:T(8,128)S(1)}, f32[2,1024,256]{2,1,0:T(8,128)}, u32[]{:S(2)}) copy-start(f32[2,1024,256]{2,1,0:T(8,128)} %y_ref.4) | copy-start | bytes 6291460
  10.2 11.6 %copy-start.10 = (f32[2,1,256,256]{3,2,1,0:T(8,128)S(1)}, f32[2,1,256,256]{3,2,1,0:T(8,128)}, u32[]{:S(2)}) copy-start(f32[2,1,256,256]{3,2,1,0:T(8,128)} %param.16) | copy-start | bytes 1572868
  16.3 28.1 %collective-permute-start.4 = (f32[256,512]{1,0:T(8,128)S(1)}, f32[256,512]{1,0:T(8,128)S(1)}, u32[]{:S(2)}, u32[]{:S(2)}) collective-permute-start(f32[256,512]{1,0:T(8,128)S(1)} %get-tuple-element.55.refs_4_.refs_0_), channel_id=1, source_target_pairs={{0,1},{2,3},{4,5},{6,7},{8,9},{10,11},{12,13},{14,15},{16,17},{18,... | collective-permute-start | bytes 1572872 | tf_op jit(solution)/shard_map/ppermute | solution.py:299
  20.4 7.2 %collective-permute-start.5 = (f32[2,128,256]{2,1,0:T(8,128)S(1)}, f32[2,128,256]{2,1,0:T(8,128)S(1)}, u32[]{:S(2)}, u32[]{:S(2)}) collective-permute-start(f32[2,128,256]{2,1,0:T(8,128)S(1)} %get-tuple-element.56.rest_0_), channel_id=1, source_target_pairs={{2,1},{6,5},{10,9},{14,13},{18,17},{22,21},{26,25},{30,29},{34,33}... | collective-permute-start | bytes 786440 | tf_op jit(solution)/shard_map/ppermute | solution.py:534
  21.1 6.5 %collective-permute-start.6 = (f32[2,128,256]{2,1,0:T(8,128)S(1)}, f32[2,128,256]{2,1,0:T(8,128)S(1)}, u32[]{:S(2)}, u32[]{:S(2)}) collective-permute-start(f32[2,128,256]{2,1,0:T(8,128)S(1)} %get-tuple-element.59), channel_id=1, source_target_pairs={{2,3},{6,7},{10,11},{14,15},{18,19},{22,23},{26,27},{30,31},{34,35... | collective-permute-start | bytes 786440 | tf_op jit(solution)/shard_map/ppermute | solution.py:534
  21.8 20.0 %copy-start.6 = (f32[1,1,256,256]{3,2,1,0:T(8,128)S(1)}, f32[1,1,256,256]{3,2,1,0:T(8,128)}, u32[]{:S(2)}) copy-start(f32[1,1,256,256]{3,2,1,0:T(8,128)} %param.27) | copy-start | bytes 786436
  28.2 18.4 %collective-permute-start.8 = (f32[2,128,256]{2,1,0:T(8,128)S(1)}, f32[2,128,256]{2,1,0:T(8,128)S(1)}, u32[]{:S(2)}, u32[]{:S(2)}) collective-permute-start(f32[2,128,256]{2,1,0:T(8,128)S(1)} %get-tuple-element.63), channel_id=1, source_target_pairs={{1,0},{3,2},{5,4},{7,6},{9,8},{11,10},{13,12},{15,14},{17,16},{19,... | collective-permute-start | bytes 786440 | tf_op jit(solution)/shard_map/ppermute | solution.py:485
  29.5 36.0 %collective-permute-start.7 = (f32[256,512]{1,0:T(8,128)S(1)}, f32[256,512]{1,0:T(8,128)S(1)}, u32[]{:S(2)}, u32[]{:S(2)}) collective-permute-start(f32[256,512]{1,0:T(8,128)S(1)} %get-tuple-element.60.refs_4_.refs_1_), channel_id=1, source_target_pairs={{0,1},{2,3},{4,5},{6,7},{8,9},{10,11},{12,13},{14,15},{16,17},{18,... | collective-permute-start | bytes 1572872 | tf_op jit(solution)/shard_map/ppermute | solution.py:299
  41.8 37.9 %collective-permute-start.13 = (f32[1,256,256]{2,1,0:T(8,128)S(1)}, f32[1,256,256]{2,1,0:T(8,128)S(1)}, u32[]{:S(2)}, u32[]{:S(2)}) collective-permute-start(f32[1,256,256]{2,1,0:T(8,128)S(1)} %bitcast.41), channel_id=1, source_target_pairs={{1,0},{3,2},{5,4},{7,6},{9,8},{11,10},{13,12},{15,14},{17,16},{19,... | collective-permute-start | bytes 786440 | tf_op jit(solution)/shard_map/ppermute | solution.py:222
  43.1 39.5 %collective-permute-start.14 = (f32[1,256,256]{2,1,0:T(8,128)S(1)}, f32[1,256,256]{2,1,0:T(8,128)S(1)}, u32[]{:S(2)}, u32[]{:S(2)}) collective-permute-start(f32[1,256,256]{2,1,0:T(8,128)S(1)} %bitcast.42), channel_id=1, source_target_pairs={{2,0},{6,4},{10,8},{14,12},{18,16},{22,20},{26,24},{30,28},{34,32}... | collective-permute-start | bytes 786440 | tf_op jit(solution)/shard_map/ppermute | solution.py:222
  44.4 21.0 %copy-start.19 = (s32[8]{0:T(128)S(1)}, s32[8]{0:T(128)}, u32[]{:S(2)}) copy-start(s32[8]{0:T(128)} %param.21) | copy-start | bytes 100
  44.4 21.0 %copy-start.20 = (s32[16,1]{0,1:T(1,128)S(1)}, s32[16,1]{0,1:T(1,128)}, u32[]{:S(2)}) copy-start(s32[16,1]{0,1:T(1,128)} %param.20) | copy-start | bytes 196
  44.4 22.4 %copy-start.18 = (s32[16,128]{1,0:T(8,128)S(1)}, s32[16,128]{1,0:T(8,128)}, u32[]{:S(2)}) copy-start(s32[16,128]{1,0:T(8,128)} %param.22) | copy-start | bytes 24580
  45.1 30.3 %collective-permute-start.10 = (f32[256,512]{1,0:T(8,128)}, f32[256,512]{1,0:T(8,128)}, u32[]{:S(2)}, u32[]{:S(2)}) collective-permute-start(f32[256,512]{1,0:T(8,128)} %get-tuple-element.64.refs_2_), channel_id=1, source_target_pairs={{3,2},{7,6},{11,10},{15,14},{19,18},{23,22},{27,26},{31,30},{35,34... | collective-permute-start | bytes 1572872 | tf_op jit(solution)/shard_map/ppermute | solution.py:304
  46.5 28.8 %collective-permute-start.9 = (f32[256,512]{1,0:T(8,128)}, f32[256,512]{1,0:T(8,128)}, u32[]{:S(2)}, u32[]{:S(2)}) collective-permute-start(f32[256,512]{1,0:T(8,128)} %get-tuple-element.64.refs_2_), channel_id=1, source_target_pairs={{1,2},{5,6},{9,10},{13,14},{17,18},{21,22},{25,26},{29,30},{33,34}... | collective-permute-start | bytes 1572872 | tf_op jit(solution)/shard_map/ppermute | solution.py:303
  49.8 18.1 %copy-start.5 = (f32[1,1,256,256]{3,2,1,0:T(8,128)S(1)}, f32[1,1,256,256]{3,2,1,0:T(8,128)}, u32[]{:S(2)}) copy-start(f32[1,1,256,256]{3,2,1,0:T(8,128)} %param.26) | copy-start | bytes 786436
  49.8 18.1 %copy-start.16 = (f32[1,1,256,256]{3,2,1,0:T(8,128)S(1)}, f32[1,1,256,256]{3,2,1,0:T(8,128)}, u32[]{:S(2)}) copy-start(f32[1,1,256,256]{3,2,1,0:T(8,128)} %param.25) | copy-start | bytes 786436
  49.8 27.0 %all-to-all-start = ((f32[16,2,8,512]{3,2,1,0:T(8,128)}), f32[16,2,8,512]{3,2,1,0:T(8,128)}, u32[]{:S(2)}, u32[]{:S(2)}) async-start(f32[16,2,8,512]{3,2,1,0:T(8,128)} %map_rows.1.refs_0_), calls=%async_computation | async-start | bytes 1048576 | tf_op jit(solution)/shard_map/all_to_all | solution.py:490
  65.5 17.8 %collective-permute-start.15 = (f32[1,256,256]{2,1,0:T(8,128)S(1)}, f32[1,256,256]{2,1,0:T(8,128)S(1)}, u32[]{:S(2)}, u32[]{:S(2)}) collective-permute-start(f32[1,256,256]{2,1,0:T(8,128)S(1)} %bitcast.43), channel_id=1, source_target_pairs={{4,0},{12,8},{20,16},{28,24},{36,32},{44,40},{52,48},{60,56},{68,6... | collective-permute-start | bytes 786440 | tf_op jit(solution)/shard_map/ppermute | solution.py:222
  67.0 1.6 copy-start.11
  67.0 2.0 %copy-start.12 = (f32[1,1024,256]{2,1,0:T(8,128)S(1)}, f32[1,1024,256]{2,1,0:T(8,128)}, u32[]{:S(2)}) copy-start(f32[1,1024,256]{2,1,0:T(8,128)} %y_ref.5) | copy-start | bytes 3145732
  67.8 6.7 %copy-start.15 = (f32[256,512]{1,0:T(8,128)}, f32[256,512]{1,0:T(8,128)S(1)}, u32[]{:S(2)}) copy-start(f32[256,512]{1,0:T(8,128)S(1)} %get-tuple-element.70.rest_0_) | copy-start | bytes 1572868
  74.5 0.9 copy-start.13
  76.0 0.8 copy-start.17
  76.8 32.0 %collective-permute-start.11 = (f32[256,512]{1,0:T(8,128)}, f32[256,512]{1,0:T(8,128)}, u32[]{:S(2)}, u32[]{:S(2)}) collective-permute-start(f32[256,512]{1,0:T(8,128)} %copy-done.15), channel_id=1, source_target_pairs={{1,2},{5,6},{9,10},{13,14},{17,18},{21,22},{25,26},{29,30},{33,34}... | collective-permute-start | bytes 1572872 | tf_op jit(solution)/shard_map/ppermute | solution.py:303
  78.2 30.6 %collective-permute-start.12 = (f32[256,512]{1,0:T(8,128)}, f32[256,512]{1,0:T(8,128)}, u32[]{:S(2)}, u32[]{:S(2)}) collective-permute-start(f32[256,512]{1,0:T(8,128)} %copy-done.15), channel_id=1, source_target_pairs={{3,2},{7,6},{11,10},{15,14},{19,18},{23,22},{27,26},{31,30},{35,34... | collective-permute-start | bytes 1572872 | tf_op jit(solution)/shard_map/ppermute | solution.py:304
  79.7 17.4 %collective-permute-start.16 = (f32[1,256,256]{2,1,0:T(8,128)S(1)}, f32[1,256,256]{2,1,0:T(8,128)S(1)}, u32[]{:S(2)}, u32[]{:S(2)}) collective-permute-start(f32[1,256,256]{2,1,0:T(8,128)S(1)} %bitcast.44), channel_id=1, source_target_pairs={{8,0},{24,16},{40,32},{56,48},{72,64},{88,80},{104,96},{120,112}} | collective-permute-start | bytes 786440 | tf_op jit(solution)/shard_map/ppermute | solution.py:222
  82.6 35.6 %collective-permute-start.17 = (f32[256,512]{1,0:T(8,128)}, f32[256,512]{1,0:T(8,128)S(1)}, u32[]{:S(2)}, u32[]{:S(2)}) collective-permute-start(f32[256,512]{1,0:T(8,128)} %copy-done.17), channel_id=1, source_target_pairs={{2,4},{10,12},{18,20},{26,28},{34,36},{42,44},{50,52},{58,60},{66,... | collective-permute-start | bytes 1572872 | tf_op jit(solution)/shard_map/ppermute | solution.py:303
  83.3 34.9 %collective-permute-start.18 = (f32[256,512]{1,0:T(8,128)}, f32[256,512]{1,0:T(8,128)S(1)}, u32[]{:S(2)}, u32[]{:S(2)}) collective-permute-start(f32[256,512]{1,0:T(8,128)} %copy-done.17), channel_id=1, source_target_pairs={{6,4},{14,12},{22,20},{30,28},{38,36},{46,44},{54,52},{62,60},{70,... | collective-permute-start | bytes 1572872 | tf_op jit(solution)/shard_map/ppermute | solution.py:304
  97.1 1.1 copy-start.14
  102.3 15.1 %copy-start.4 = (f32[1,1024,512]{2,1,0:T(8,128)S(1)}, f32[1,1024,512]{2,1,0:T(8,128)}, u32[]{:S(2)}) copy-start(f32[1,1024,512]{2,1,0:T(8,128)} %get-tuple-element.77.top_ref.refs_2_) | copy-start | bytes 6291460
  102.3 13.3 %collective-permute-start.19 = (f32[256,256]{1,0:T(8,128)S(1)}, f32[256,256]{1,0:T(8,128)S(1)}, u32[]{:S(2)}, u32[]{:S(2)}) collective-permute-start(f32[256,256]{1,0:T(8,128)S(1)} %get-tuple-element.78.send_ref), channel_id=1, source_target_pairs={{0,1},{1,0},{2,3},{3,2},{4,5},{5,4},{6,7},{7,6},{8,9},{9,8},{10,11... | collective-permute-start | bytes 786440 | tf_op jit(solution)/shard_map/ppermute | solution.py:217
  109.4 25.2 %collective-permute-start.20 = (f32[256,512]{1,0:T(8,128)S(1)}, f32[256,512]{1,0:T(8,128)S(1)}, u32[]{:S(2)}, u32[]{:S(2)}) collective-permute-start(f32[256,512]{1,0:T(8,128)S(1)} %get-tuple-element.79.outs_0_), channel_id=1, source_target_pairs={{2,4},{10,12},{18,20},{26,28},{34,36},{42,44},{50,52},{58,60},{66,... | collective-permute-start | bytes 1572872 | tf_op jit(solution)/shard_map/ppermute | solution.py:303
  110.1 24.5 %collective-permute-start.21 = (f32[256,512]{1,0:T(8,128)S(1)}, f32[256,512]{1,0:T(8,128)S(1)}, u32[]{:S(2)}, u32[]{:S(2)}) collective-permute-start(f32[256,512]{1,0:T(8,128)S(1)} %get-tuple-element.79.outs_0_), channel_id=1, source_target_pairs={{6,4},{14,12},{22,20},{30,28},{38,36},{46,44},{54,52},{62,60},{70,... | collective-permute-start | bytes 1572872 | tf_op jit(solution)/shard_map/ppermute | solution.py:304
  115.6 8.0 %collective-permute-start.22 = (f32[256,256]{1,0:T(8,128)S(1)}, f32[256,256]{1,0:T(8,128)S(1)}, u32[]{:S(2)}, u32[]{:S(2)}) collective-permute-start(f32[256,256]{1,0:T(8,128)S(1)} %get-tuple-element.74.refs_1_.send_ref), channel_id=1, source_target_pairs={{0,1},{1,0},{2,3},{3,2},{4,5},{5,4},{6,7},{7,6},{8,9},{9,8},{10,11... | collective-permute-start | bytes 786440 | tf_op jit(solution)/shard_map/ppermute | solution.py:217
  118.9 24.9 %collective-permute-start.23 = (f32[256,512]{1,0:T(8,128)S(1)}, f32[256,512]{1,0:T(8,128)S(1)}, u32[]{:S(2)}, u32[]{:S(2)}) collective-permute-start(f32[256,512]{1,0:T(8,128)S(1)} %get-tuple-element.82.outs_0_), channel_id=1, source_target_pairs={{4,8},{20,24},{36,40},{52,56},{68,72},{84,88},{100,104},{116,120}} | collective-permute-start | bytes 1572872 | tf_op jit(solution)/shard_map/ppermute | solution.py:303
  119.6 25.9 %collective-permute-start.24 = (f32[256,512]{1,0:T(8,128)S(1)}, f32[256,512]{1,0:T(8,128)S(1)}, u32[]{:S(2)}, u32[]{:S(2)}) collective-permute-start(f32[256,512]{1,0:T(8,128)S(1)} %get-tuple-element.82.outs_0_), channel_id=1, source_target_pairs={{12,8},{28,24},{44,40},{60,56},{76,72},{92,88},{108,104},{124,120}} | collective-permute-start | bytes 1572872 | tf_op jit(solution)/shard_map/ppermute | solution.py:304
  123.5 16.1 %collective-permute-start.25 = (f32[256,256]{1,0:T(8,128)S(1)}, f32[256,256]{1,0:T(8,128)S(1)}, u32[]{:S(2)}, u32[]{:S(2)}) collective-permute-start(f32[256,256]{1,0:T(8,128)S(1)} %get-tuple-element.85.send_ref), channel_id=1, source_target_pairs={{0,2},{1,3},{2,0},{3,1},{4,6},{5,7},{6,4},{7,5},{8,10},{9,11},{10,... | collective-permute-start | bytes 786440 | tf_op jit(solution)/shard_map/ppermute | solution.py:217
  135.4 15.5 %collective-permute-start.27 = (f32[256,512]{1,0:T(8,128)S(1)}, f32[256,512]{1,0:T(8,128)S(1)}, u32[]{:S(2)}, u32[]{:S(2)}) collective-permute-start(f32[256,512]{1,0:T(8,128)S(1)} %get-tuple-element.86.outs_0_), channel_id=1, source_target_pairs={{4,8},{20,24},{36,40},{52,56},{68,72},{84,88},{100,104},{116,120}} | collective-permute-start | bytes 1572872 | tf_op jit(solution)/shard_map/ppermute | solution.py:303
  136.1 14.8 %collective-permute-start.28 = (f32[256,512]{1,0:T(8,128)S(1)}, f32[256,512]{1,0:T(8,128)S(1)}, u32[]{:S(2)}, u32[]{:S(2)}) collective-permute-start(f32[256,512]{1,0:T(8,128)S(1)} %get-tuple-element.86.outs_0_), channel_id=1, source_target_pairs={{12,8},{28,24},{44,40},{60,56},{76,72},{92,88},{108,104},{124,120}} | collective-permute-start | bytes 1572872 | tf_op jit(solution)/shard_map/ppermute | solution.py:304
  139.7 8.7 %collective-permute-start.29 = (f32[256,256]{1,0:T(8,128)S(1)}, f32[256,256]{1,0:T(8,128)S(1)}, u32[]{:S(2)}, u32[]{:S(2)}) collective-permute-start(f32[256,256]{1,0:T(8,128)S(1)} %get-tuple-element.90.send_ref), channel_id=1, source_target_pairs={{0,2},{1,3},{2,0},{3,1},{4,6},{5,7},{6,4},{7,5},{8,10},{9,11},{10,... | collective-permute-start | bytes 786440 | tf_op jit(solution)/shard_map/ppermute | solution.py:217
  143.8 8.5 %collective-permute-start.31 = (f32[256,256]{1,0:T(8,128)S(1)}, f32[256,256]{1,0:T(8,128)S(1)}, u32[]{:S(2)}, u32[]{:S(2)}) collective-permute-start(f32[256,256]{1,0:T(8,128)S(1)} %get-tuple-element.94.send_ref), channel_id=1, source_target_pairs={{0,4},{1,5},{2,6},{3,7},{4,0},{5,1},{6,2},{7,3},{8,12},{9,13},{10,... | collective-permute-start | bytes 786440 | tf_op jit(solution)/shard_map/ppermute | solution.py:217
  149.3 13.1 %collective-permute-start.33 = (f32[256,256]{1,0:T(8,128)S(1)}, f32[256,256]{1,0:T(8,128)S(1)}, u32[]{:S(2)}, u32[]{:S(2)}) collective-permute-start(f32[256,256]{1,0:T(8,128)S(1)} %get-tuple-element.97.send_ref), channel_id=1, source_target_pairs={{0,4},{1,5},{2,6},{3,7},{4,0},{5,1},{6,2},{7,3},{8,12},{9,13},{10,... | collective-permute-start | bytes 786440 | tf_op jit(solution)/shard_map/ppermute | solution.py:217
  153.2 17.5 %collective-permute-start.32 = (f32[256,256]{1,0:T(8,128)S(1)}, f32[256,256]{1,0:T(8,128)S(1)}, u32[]{:S(2)}, u32[]{:S(2)}) collective-permute-start(f32[256,256]{1,0:T(8,128)S(1)} %get-tuple-element.96.send_ref), channel_id=1, source_target_pairs={{0,8},{1,9},{2,10},{3,11},{4,12},{5,13},{6,14},{7,15},{8,0},{9,1},... | collective-permute-start | bytes 786440 | tf_op jit(solution)/shard_map/ppermute | solution.py:217
  163.4 11.3 %collective-permute-start.34 = (f32[256,256]{1,0:T(8,128)S(1)}, f32[256,256]{1,0:T(8,128)S(1)}, u32[]{:S(2)}, u32[]{:S(2)}) collective-permute-start(f32[256,256]{1,0:T(8,128)S(1)} %get-tuple-element.99.send_ref), channel_id=1, source_target_pairs={{0,8},{1,9},{2,10},{3,11},{4,12},{5,13},{6,14},{7,15},{8,0},{9,1},... | collective-permute-start | bytes 786440 | tf_op jit(solution)/shard_map/ppermute | solution.py:217
  168.1 12.6 %collective-permute-start.26 = (f32[128,512]{1,0:T(8,128)S(1)}, f32[128,512]{1,0:T(8,128)S(1)}, u32[]{:S(2)}, u32[]{:S(2)}) collective-permute-start(f32[128,512]{1,0:T(8,128)S(1)} %get-tuple-element.88.outs_0_), channel_id=1, source_target_pairs={{8,0},{24,16},{40,32},{56,48},{72,64},{88,80},{104,96},{120,112}} | collective-permute-start | bytes 786440 | tf_op jit(solution)/shard_map/ppermute | solution.py:518
  169.4 14.3 %collective-permute-start.30 = (f32[128,512]{1,0:T(8,128)S(1)}, f32[128,512]{1,0:T(8,128)S(1)}, u32[]{:S(2)}, u32[]{:S(2)}) collective-permute-start(f32[128,512]{1,0:T(8,128)S(1)} %get-tuple-element.92.outs_0_), channel_id=1, source_target_pairs={{8,0},{24,16},{40,32},{56,48},{72,64},{88,80},{104,96},{120,112}} | collective-permute-start | bytes 786440 | tf_op jit(solution)/shard_map/ppermute | solution.py:518
where the time goes:
time: 186 us; the launch traced here: 185 us
  starting transfers between devices  94.7 us (51%)
  Pallas kernels  43.7 us (23%)
  waiting for transfers between devices  22.5 us (12%)
  blocking collectives  13.1 us (7%)
  local copies, waits for them, and re-layouts  9.53 us (5%)
    ppermute x8, starting transfers between devices, exchange(): return lax.ppermute(value, 'rows', [(i, i ^ 1 << level) for i in range(16)])  38.7 us
    ppermute x2, starting transfers between devices, lead_moves(): lax.ppermute(value, 'rows', [(i, i + 1) for i in range(0, 16, 2)])  15.8 us
    ppermute x8, waiting for transfers between devices, exchange(): return lax.ppermute(value, 'rows', [(i, i ^ 1 << level) for i in range(16)])  15.7 us
    all_to_all x1, starting transfers between devices, per_device(): swapped = lax.all_to_all(pieces, 'rows', 0, 0)  15.6 us
    all_gather x1, blocking collectives, per_device(): portion = lax.all_gather(mine, 'fronts', axis=0, tiled=True)  13.1 us
    pallas_call x2, Pallas kernels, block_step(): pl.pallas_call(kernel, grid_spec=pltpu.PrefetchScalarGridSpec(num_scalar_...  11.9 us
    unnamed x42, local copies, waits for them, and re-layouts  8.71 us
    pallas_call x8, Pallas kernels, tree_level(): pl.pallas_call(kernel, grid_spec=pltpu.PrefetchScalarGridSpec(num_scalar_...  7.21 us
  transfers between devices with their start and end apart: 36, of which 7 were waited for; matrix products, arithmetic and copies ran while one was open for 0% of the time, Pallas kernels for 22%

commit v1 on v0

--- a/solution.py
+++ b/solution.py
@@ -15,6 +15,7 @@
 F32 = jnp.float32
 BF16 = jnp.bfloat16
 HBM = pl.BlockSpec(memory_space=pl.ANY)
+FAR = pl.BlockSpec(memory_space=pltpu.HBM)
 
 
 NN = ((1,), (0,))
@@ -41,8 +42,8 @@
     return pl.BlockSpec(shape, lambda *_: index)
 
 
-def params():
-    return pltpu.CompilerParams(vmem_limit_bytes=48 * 1024 * 1024)
+def params(mebibytes=48):
+    return pltpu.CompilerParams(vmem_limit_bytes=mebibytes * 1024 * 1024)
 
 
 def role(info, live_at, level):
@@ -55,23 +56,57 @@
     return lead, rest
 
 
+def row_copies(source, target, sems, at):
+    part = [pl.ds(c * K, K) for c in range(BR // K)]
+    return [pltpu.make_async_copy(source.at[p], target.at[p], sems.at[at, c]) for c, p in enumerate(part)]
+
+
+def start_all(*copies):
+    for group in zip(*copies):
+        for copy in group:
+            copy.start()
+
+
+def wait_all(copies):
+    for copy in copies:
+        copy.wait()
+
+
 def block_step(info, live_at, front, rhs, vectors, factors, prior, after=()):
-    def kernel(info, x_ref, y_ref, g_ref, *rest):
-        out_ref, top_ref = rest[-2:]
+    def kernel(info, x_hbm, y_hbm, g_hbm, *rest):
+        out_hbm, top_hbm, x, y, g, sems = rest[-6:]
         active = info[0] < info[live_at]
+        x_in = row_copies(x_hbm.at[front], x, sems, 0)
+        y_in = row_copies(y_hbm.at[front], y, sems, 1)
+        out = row_copies(x, out_hbm.at[front], sems, 2)
+        g_in = pltpu.make_async_copy(g_hbm.at[front], g, sems.at[3, 0])
+        top = pltpu.make_async_copy(x.at[pl.ds(0, K)], top_hbm, sems.at[3, 1])
+        start_all(y_in, x_in)
+        g_in.start()
 
         @pl.when(active)
         def _():
-            x, y = x_ref[0], y_ref[0]
-            project = dot3(split(y.T), split(x), NN)
-            scaled = dot3(split(g_ref[0].T), split(project), NN)
-            out_ref[0] = x - dot3(split(y), split(scaled), NN)
+            project = jnp.zeros((K, N), F32)
+            for c in range(BR // K):
+                y_in[c].wait()
+                x_in[c].wait()
+                part = slice(c * K, (c + 1) * K)
+                project = project + dot3(split(y[part].T), split(x[part]), NN)
+            g_in.wait()
+            scaled = split(dot3(split(g[...].T), split(project), NN))
+            for c in range(BR // K):
+                part = slice(c * K, (c + 1) * K)
+                x[part] = x[part] - dot3(split(y[part]), scaled, NN)
+                out[c].start()
+                if c == 0:
+                    top.start()
 
         @pl.when(jnp.logical_not(active))
         def _():
-            out_ref[0] = x_ref[0]
-
-        top_ref[...] = out_ref[0, :K]
+            wait_all(y_in + x_in + [g_in])
+            start_all(out + [top])
+
+        wait_all(out + [top])
 
     operands = [info, rhs, vectors, factors, *after] + ([] if prior is None else [prior])
     return pl.pallas_call(
@@ -79,59 +114,90 @@
         grid_spec=pltpu.PrefetchScalarGridSpec(
             num_scalar_prefetch=1,
             grid=(1,),
-            in_specs=[
-                spec((1, BR, N), (front, 0, 0)),
-                spec((1, BR, K), (front, 0, 0)),
-                spec((1, K, K), (front, 0, 0)),
-            ]
-            + [HBM] * (len(operands) - 4),
-            out_specs=[spec((1, BR, N), (front, 0, 0)), full((K, N))],
+            in_specs=[FAR] * 3 + [HBM] * (len(operands) - 4),
+            out_specs=[HBM, HBM],
+            scratch_shapes=[
+                pltpu.VMEM((BR, N), F32),
+                pltpu.VMEM((BR, K), F32),
+                pltpu.VMEM((K, K), F32),
+                pltpu.SemaphoreType.DMA((4, BR // K)),
+            ],
         ),
         out_shape=[jax.ShapeDtypeStruct(rhs.shape, F32), jax.ShapeDtypeStruct((K, N), F32)],
         input_output_aliases={} if prior is None else {len(operands) - 1: 0},
-        compiler_params=params(),
+        compiler_params=params(60),
     )(*operands)
 
 
 def parent_before(info, rhs, vectors, factors, node_vectors, rows, after=()):
-    def kernel(info, x_ref, y_ref, g_ref, v_ref, rows_ref, *rest):
-        out_ref, unit_ref, send_ref, wide = rest[-4:]
-        chosen = lax.broadcasted_iota(jnp.int32, (BR, CB), 0) == rows_ref[0:1, :]
-        chosen = jnp.where(chosen, 1.0, 0.0)
-        taken = jnp.max(chosen, axis=1, keepdims=True) > 0.5
-        wide[:, :N] = jnp.where(taken, 0.0, x_ref[0])
-        wide[:, N:] = chosen
-        y = y_ref[0]
-        project = dot3(split(y.T), split(wide[...]), NN)
-        scaled = dot3(split(g_ref[0].T), split(project), NN)
-        wide[...] = wide[...] - dot3(split(y), split(scaled), NN)
-        out_ref[0] = wide[:, :N]
-        unit_ref[...] = wide[:, N:]
+    def kernel(info, x_hbm, y_hbm, g_hbm, v_hbm, rows_ref, *rest):
+        out_hbm, unit_ref, send_ref, x, y, g, v, sems = rest[-8:]
+        x_in = row_copies(x_hbm.at[0], x, sems, 0)
+        y_in = row_copies(y_hbm.at[0], y, sems, 1)
+        out = row_copies(x, out_hbm.at[0], sems, 2)
+        g_in = pltpu.make_async_copy(g_hbm.at[0], g, sems.at[3, 0])
+        v_in = pltpu.make_async_copy(v_hbm.at[0], v, sems.at[3, 1])
+        start_all(y_in, x_in)
+        start_all([g_in, v_in])
+        project = jnp.zeros((K, N), F32)
+        project_unit = jnp.zeros((K, CB), F32)
+        for c in range(BR // K):
+            part = slice(c * K, (c + 1) * K)
+            chosen = lax.broadcasted_iota(jnp.int32, (K, CB), 0) + c * K == rows_ref[0:1, :]
+            chosen = jnp.where(chosen, 1.0, 0.0)
+            taken = jnp.max(chosen, axis=1, keepdims=True) > 0.5
+            unit_ref[part] = chosen
+            y_in[c].wait()
+            x_in[c].wait()
+            x[part] = jnp.where(taken, 0.0, x[part])
+            turned = split(y[part].T)
+            project = project + dot3(turned, split(x[part]), NN)
+            project_unit = project_unit + dot3(turned, split(chosen), NN)
+        wait_all([g_in, v_in])
+        turned = split(g[...].T)
+        scaled = split(dot3(turned, split(project), NN))
+        scaled_unit = split(dot3(turned, split(project_unit), NN))
+        for c in range(BR // K):
+            part = slice(c * K, (c + 1) * K)
+            high_low = split(y[part])
+            x[part] = x[part] - dot3(high_low, scaled, NN)
+            out[c].start()
+            unit_ref[part] = unit_ref[part] - dot3(high_low, scaled_unit, NN)
 
         @pl.when(info[0] % 2 == 1)
         def _():
-            send_ref[...] = dot3(split(v_ref[0].T), split(wide[:K]), NN)
+            turned = split(v[...].T)
+            send_ref[:, :N] = dot3(turned, split(x[:K]), NN)
+            send_ref[:, N:] = dot3(turned, split(unit_ref[:K]), NN)
 
         @pl.when(info[0] % 2 == 0)
         def _():
-            send_ref[...] = wide[:K]
-
-    return pl.pallas_call(
-        kernel,
-        grid_spec=pltpu.PrefetchScalarGridSpec(
-            num_scalar_prefetch=1,
-            grid=(1,),
-            in_specs=[full((1, BR, N)), full((1, BR, K)), full((1, K, K)), full((1, K, K)), full(rows.shape)]
-            + [HBM] * len(after),
-            out_specs=[full((1, BR, N)), full((BR, CB)), full((K, N + CB))],
-            scratch_shapes=[pltpu.VMEM((BR, N + CB), F32)],
+            send_ref[:, :N] = x[:K]
+            send_ref[:, N:] = unit_ref[:K]
+
+        wait_all(out)
+
+    return pl.pallas_call(
+        kernel,
+        grid_spec=pltpu.PrefetchScalarGridSpec(
+            num_scalar_prefetch=1,
+            grid=(1,),
+            in_specs=[FAR] * 4 + [full(rows.shape)] + [HBM] * len(after),
+            out_specs=[HBM, full((BR, CB)), full((K, N + CB))],
+            scratch_shapes=[
+                pltpu.VMEM((BR, N), F32),
+                pltpu.VMEM((BR, K), F32),
+                pltpu.VMEM((K, K), F32),
+                pltpu.VMEM((K, K), F32),
+                pltpu.SemaphoreType.DMA((4, BR // K)),
+            ],
         ),
         out_shape=[
             jax.ShapeDtypeStruct(rhs.shape, F32),
             jax.ShapeDtypeStruct((BR, CB), F32),
             jax.ShapeDtypeStruct((K, N + CB), F32),
         ],
-        compiler_params=params(),
+        compiler_params=params(60),
         name="parent_before",
     )(info, rhs, vectors, factors, node_vectors, rows, *after)
 
@@ -408,29 +474,35 @@
     )(info, *ins, node_vectors, node_factors, *after)
 
 
-def map_rows(info, lead_map, rest_map, *tops, after=()):
+def map_rows(info, lead_map, rest_map, *tops):
     fronts = len(tops)
 
     def kernel(info, lead_ref, rest_ref, *refs):
         top_refs, out_ref = refs[:fronts], refs[-1]
         odd = info[0] % 2 == 1
-        for f in range(fronts):
-            chosen = jnp.where(odd, rest_ref[f], lead_ref[f])
-            product = dot3(split(chosen), split(top_refs[f][...]), NN)
-            out_ref[:, f] = product.reshape(16, CB // 16, N)
-
-    return pl.pallas_call(
-        kernel,
-        grid_spec=pltpu.PrefetchScalarGridSpec(
-            num_scalar_prefetch=1,
-            grid=(1,),
-            in_specs=[full((fronts, CB, K))] * 2 + [full((K, N))] * fronts + [HBM] * len(after),
+
+        @pl.when(odd)
+        def _():
+            for f in range(fronts):
+                product = dot3(split(lead_ref[f] + rest_ref[f]), split(top_refs[f][...]), NN)
+                out_ref[:, f] = product.reshape(16, CB // 16, N)
+
+        @pl.when(jnp.logical_not(odd))
+        def _():
+            out_ref[...] = jnp.zeros(out_ref.shape, F32)
+
+    return pl.pallas_call(
+        kernel,
+        grid_spec=pltpu.PrefetchScalarGridSpec(
+            num_scalar_prefetch=1,
+            grid=(1,),
+            in_specs=[full((fronts, CB, K))] * 2 + [full((K, N))] * fronts,
             out_specs=full((16, fronts, CB // 16, N)),
         ),
         out_shape=jax.ShapeDtypeStruct((16, fronts, CB // 16, N), F32),
         compiler_params=params(),
         name="map_rows",
-    )(info, lead_map, rest_map, *tops, *after)
+    )(info, lead_map, rest_map, *tops)
 
 
 def per_device(
@@ -475,41 +547,36 @@
     maps = maps_move(maps, [(4, 2), (12, 10)], [(4, 6), (12, 14)])
     applied, top_a = block_step(info, 1, 0, *blocks_in, None, [token])
     in_a = lead_moves(top_a, 0)
-    maps = map_node(info, 1, *maps, *nodes, [top_a])
+    applied, top_b = block_step(info, 2, 1, *blocks_in, applied)
+    in_b = lead_moves(top_b, 0)
+    maps = map_node(info, 1, *maps, *nodes, [top_b])
     token = maps[0]
     at = range(2, 16, 4)
     maps = maps_move(maps, [(i, i - 1) for i in at], [(i, i + 1) for i in at])
-    applied, top_b = block_step(info, 2, 1, *blocks_in, applied, [token])
-    in_b = lead_moves(top_b, 0)
-    maps = map_node(info, 0, *maps, *nodes, [top_b])
-    lead_map = lax.ppermute(maps[0], "rows", [(i + 1, i) for i in range(0, 16, 2)])
-    applied, lead_a = node_level(info, 1, 0, 0, applied, *in_a, *nodes, [maps[1]])
+    upper, unit, send = parent_before(info, upper_rhs, upper_vectors, upper_factors, summit_vectors, rows_here, [token])
+    applied, lead_a = node_level(info, 1, 0, 0, applied, *in_a, *nodes, [unit])
     in_a = lead_moves(lead_a, 1)
-
-    pieces = map_rows(info, lead_map, maps[1], top_a, top_b, after=[lead_a])
+    applied, lead_b = node_level(info, 2, 0, 1, applied, *in_b, *nodes, [lead_a])
+    in_b = lead_moves(lead_b, 1)
+
+    pieces = map_rows(info, *maps, lead_a, lead_b)
     swapped = lax.all_to_all(pieces, "rows", 0, 0)
-    applied, lead_b = node_level(info, 2, 0, 1, applied, *in_b, *nodes, [pieces])
-    upper, unit, send = parent_before(
-        info, upper_rhs, upper_vectors, upper_factors, summit_vectors, rows_here, [lead_b]
-    )
-    applied, lead_a = node_level(info, 1, 1, 0, applied, *in_a, *nodes, [unit])
-    swapped, lead_a, lead_b = lax.optimization_barrier((swapped, lead_a, lead_b))
-    in_b = lead_moves(lead_b, 1)
+    applied, lead_a = node_level(info, 1, 1, 0, applied, *in_a, *nodes, [pieces])
     in_a = lead_moves(lead_a, 2)
+    applied, lead_b = node_level(info, 2, 1, 1, applied, *in_b, *nodes)
+    in_b = lead_moves(lead_b, 2)
     mine = add_all(swapped)
     portion = lax.all_gather(mine, "fronts", axis=0, tiled=True)
 
     upper, *sends = parent_after(upper, unit, send, portion, lead_factors)
     half = N // 2
     chunks = [[upper, spec((1, K, half), (0, 0, j)), sends[j]] for j in range(2)]
-    lower_steps = list(LOWER_STEPS)
     order = sends[1]
     ins = {"a": in_a, "b": in_b}
     for level in range(LEVELS):
         recvs = [exchange(chunks[j][2], level) for j in range(2)]
         for j in range(2):
-            if lower_steps:
-                name, at = lower_steps.pop(0)
+            for name, at in LOWER_STEPS.get((level, j), ()):
                 f = "ab".index(name)
                 applied, order = node_level(info, 1 + f, at, f, applied, *ins[name], *nodes, [order])
                 if at < LEVELS - 1:
@@ -544,7 +611,7 @@
     return pl.pallas_call(kernel, out_shape=jax.ShapeDtypeStruct(pieces.shape[1:], F32), name="add_all")(pieces)
 
 
-LOWER_STEPS = (("b", 1), ("a", 2), ("b", 2), ("a", 3), ("b", 3))
+LOWER_STEPS = {(0, 0): (("a", 2), ("b", 2)), (0, 1): (("a", 3),), (1, 1): (("b", 3),)}
 
 
 def solution(mesh):

time: 186 us -> 219 us (1.18)
  waiting for transfers between devices: 22.5 us -> 43 us
  starting transfers between devices: 94.7 us -> 103 us
  local copies, waits for them, and re-layouts: 9.53 us -> 6.35 us
  blocking collectives: 13.1 us -> 16.2 us
  Pallas kernels: 43.7 us -> 46.2 us
    all_to_all x1, starting transfers between devices: 15.6 us -> 49.3 us  [per_device(): swapped = lax.all_to_all(pieces, 'rows', 0, 0)]
    ppermute x4, waiting for transfers between devices: 0.01 us -> 16.3 us  [lead_gets(): lax.ppermute(value, 'rows', [(b + step, b) for b in range(0, 16, 2 * step)])]
    ppermute x8, starting transfers between devices: 38.7 us -> 23.2 us  [exchange(): return lax.ppermute(value, 'rows', [(i, i ^ 1 << level) for i in range(16)])]
    ppermute x2, starting transfers between devices: 15.8 us -> 4.85 us  [lead_moves(): lax.ppermute(value, 'rows', [(i, i + 1) for i in range(0, 16, 2)])]
    unnamed x42, local copies, waits for them, and re-layouts: 8.71 us -> 4.94 us
    pallas_call x1, Pallas kernels: 5.43 us -> 8.63 us  [parent_before(): pl.pallas_call(kernel, grid_spec=pltpu.PrefetchScalarGridSpec(num_scalar_...]
    all_gather x1, blocking collectives: 13.1 us -> 16.2 us  [per_device(): portion = lax.all_gather(mine, 'fronts', axis=0, tiled=True)]
    ppermute x2, waiting for transfers between devices: 0.01 us -> 2.66 us  [lead_moves(): lax.ppermute(value, 'rows', [(i, i + 1) for i in range(0, 16, 2)])]
  transfers between devices with their start and end apart: 36 -> 35, of which waited for: 7 -> 10; matrix products, arithmetic and copies ran while one was open for 0% -> 0% of each run, Pallas kernels for 22% -> 15%
where the time goes in v1:
time: 219 us; the launch traced here: 216 us
  starting transfers between devices  103 us (47%)
  Pallas kernels  46.2 us (21%)
  waiting for transfers between devices  43 us (20%)
  blocking collectives  16.2 us (7%)
  local copies, waits for them, and re-layouts  6.35 us (3%)
    all_to_all x1, starting transfers between devices, per_device(): swapped = lax.all_to_all(pieces, 'rows', 0, 0)  49.3 us
    ppermute x8, starting transfers between devices, exchange(): return lax.ppermute(value, 'rows', [(i, i ^ 1 << level) for i in range(16)])  23.2 us
    ppermute x4, waiting for transfers between devices, lead_gets(): lax.ppermute(value, 'rows', [(b + step, b) for b in range(0, 16, 2 * step)])  16.3 us
    all_gather x1, blocking collectives, per_device(): portion = lax.all_gather(mine, 'fronts', axis=0, tiled=True)  16.2 us
    ppermute x8, waiting for transfers between devices, exchange(): return lax.ppermute(value, 'rows', [(i, i ^ 1 << level) for i in range(16)])  16.1 us
    pallas_call x2, Pallas kernels, block_step(): pl.pallas_call(kernel, grid_spec=pltpu.PrefetchScalarGridSpec(num_scalar_...  11.2 us
    pallas_call x1, Pallas kernels, parent_before(): pl.pallas_call(kernel, grid_spec=pltpu.PrefetchScalarGridSpec(num_scalar_...  8.63 us
    ppermute x2, waiting for transfers between devices, per_device(): ins[name] = lax.ppermute(order, 'rows', [(8, 0)])  7.91 us
  transfers between devices with their start and end apart: 35, of which 10 were waited for; matrix products, arithmetic and copies ran while one was open for 0% of the time, Pallas kernels for 15%

profile of v1, /device:TPU:0, one launch (start us, length us, event | category | flops | bytes accessed | tf_op | source)
XLA Modules:
  0.0 216.1 jit_solution(16067712429849668806)
XLA Ops:
  0.6 0.7 dynamic_slice.6
  1.5 1.0 copy-done
  2.5 1.0 copy-done.2
  6.1 0.7 copy-done.14
  6.8 5.5 %shard_map.151 = (f32[2,1024,512]{2,1,0:T(8,128)}, f32[256,512]{1,0:T(8,128)}) custom-call(s32[4]{0:T(128)} %copy-done.11, f32[2,1024,512]{2,1,0:T(8,128)} %x_hbm.4, f32[2,1024,256]{2,1,0:T(8,128)} %y_hbm.4, f32[2,256,256]{2,1,0:T(8,128)} %bitcast.51, f32[2,128,256]{2,1,0:T(8,128)} %copy-done.14), custom_call_target="tpu_custom_call" | custom-call | tf_op jit(solution)/shard_map/pallas_call | solution.py:112
  12.4 5.7 %shard_map.152 = (f32[2,1024,512]{2,1,0:T(8,128)}, f32[256,512]{1,0:T(8,128)}) custom-call(s32[4]{0:T(128)} %copy-done.11, f32[2,1024,512]{2,1,0:T(8,128)} %x_hbm.4, f32[2,1024,256]{2,1,0:T(8,128)} %y_hbm.4, f32[2,256,256]{2,1,0:T(8,128)} %bitcast.52, f32[2,1024,512]{2,1,0:T(8,128)} %get-tuple-element.49.rest_0_), custom_call_target="tpu_custom_call", output_to_operand_aliasing={{0}: (4, {})} | custom-call | tf_op jit(solution)/shard_map/pallas_call | solution.py:112
  18.1 3.5 %collective-permute-start.2 = (f32[256,512]{1,0:T(8,128)}, f32[256,512]{1,0:T(8,128)S(1)}, u32[]{:S(2)}, u32[]{:S(2)}) collective-permute-start(f32[256,512]{1,0:T(8,128)} %get-tuple-element.51), channel_id=1, source_target_pairs={{0,1},{2,3},{4,5},{6,7},{8,9},{10,11},{12,13},{14,15},{16,17},{18,... | collective-permute-start | bytes 1572872 | tf_op jit(solution)/shard_map/ppermute | solution.py:365
  21.6 1.3 collective-permute-start.5
  23.7 0.7 collective-permute-start.4
  24.7 1.0 copy-done.10
  26.3 0.7 collective-permute-start.8
  27.6 8.6 %parent_before.1 = (f32[1,1024,512]{2,1,0:T(8,128)}, f32[1024,128]{1,0:T(8,128)}, f32[256,640]{1,0:T(8,128)}) custom-call(s32[4]{0:T(128)} %copy-done.11, f32[1,1024,512]{2,1,0:T(8,128)} %x_hbm.5, f32[1,1024,256]{2,1,0:T(8,128)} %y_hbm.5, f32[1,256,256]{2,1,0:T(8,128)} %bitcast.53, f32[1,256,256]{2,1,0:T(8,128)} %bitcast.30, ...), custom_call_target="tpu_custom_call" | custom-call | tf_op jit(solution)/shard_map/parent_before/pallas_call | solution.py:180
  36.2 1.0 copy-done.7
  37.9 0.8 collective-permute-start.6
  38.7 0.9 collective-permute-start.7
  39.6 0.7 collective-permute-start.9
  40.3 2.7 %collective-permute-done.5.lead_ref = f32[256,512]{1,0:T(8,128)S(1)} collective-permute-done((f32[256,512]{1,0:T(8,128)}, f32[256,512]{1,0:T(8,128)S(1)}, u32[]{:S(2)}, u32[]{:S(2)}) %collective-permute-start.5) | collective-permute-done | bytes 524320 | tf_op jit(solution)/shard_map/ppermute | solution.py:365
  43.6 1.5 collective-permute-start.10
  45.0 1.5 collective-permute-start.11
  46.5 1.3 collective-permute-start.14
  47.8 2.4 %map_rows.1.refs_1_ = f32[16,2,8,512]{3,2,1,0:T(8,128)} custom-call(s32[4]{0:T(128)S(1)} %copy-done.13, f32[2,128,256]{2,1,0:T(8,128)S(1)} %collective-permute-done.8.lead_ref, f32[2,128,256]{2,1,0:T(8,128)S(1)} %collective-permute-done.9.rest_ref, f32[256,512]{1,0:T(8,128)S(1)} %get-tuple-element.57.refs_0_, f32[256,512]{1,0:T(8,128)} %get-tuple-element.60.refs_1_), custom_call_target="tpu_custom_call" | custom-call | tf_op jit(solution)/shard_map/map_rows/pallas_call | solution.py:494
  50.3 49.3 %all-to-all-start = ((f32[16,2,8,512]{3,2,1,0:T(8,128)}), f32[16,2,8,512]{3,2,1,0:T(8,128)}, u32[]{:S(2)}, u32[]{:S(2)}) async-start(f32[16,2,8,512]{3,2,1,0:T(8,128)} %map_rows.1.refs_1_), calls=%async_computation | async-start | bytes 1048576 | tf_op jit(solution)/shard_map/all_to_all | solution.py:563
  100.2 1.6 collective-permute-start.12
  101.8 1.4 collective-permute-start.13
  103.3 1.3 collective-permute-start.15
  104.6 1.3 collective-permute-start.16
  105.9 1.3 collective-permute-start.17
  107.8 16.3 %collective-permute-done.15.rest_1_.gl_ref = f32[1,256,256]{2,1,0:T(8,128)S(1)} collective-permute-done((f32[1,256,256]{2,1,0:T(8,128)S(1)}, f32[1,256,256]{2,1,0:T(8,128)S(1)}, u32[]{:S(2)}, u32[]{:S(2)}) %collective-permute-start.15) | collective-permute-done | bytes 262176 | tf_op jit(solution)/shard_map/ppermute | solution.py:288
  124.1 1.5 collective-permute-start.18
  125.6 1.5 collective-permute-start.19
  127.1 1.7 add_all.1
  128.7 16.2 %all_gather.3.data_ref = f32[16,8,512]{2,1,0:T(8,128)S(1)} all-gather(f32[2,8,512]{2,1,0:T(8,128)} %add_all.1), channel_id=1, replica_groups=mesh['fronts'=8,'rows'=16] {'fronts'}, dimensions={0}, use_global_device_ids=true | all-gather | bytes 294912 | tf_op jit(solution)/shard_map/all_gather | solution.py:569
  145.0 4.1 %parent_after.1 = (f32[1,1024,512]{2,1,0:T(8,128)}, f32[256,256]{1,0:T(8,128)S(1)}, f32[256,256]{1,0:T(8,128)S(1)}) custom-call(f32[1,1024,512]{2,1,0:T(8,128)} %get-tuple-element.64.x_ref, f32[1024,128]{1,0:T(8,128)S(1)} %copy-done.8, f32[256,640]{1,0:T(8,128)S(1)} %copy-done.9, ...), custom_call_target="tpu_custom_call", output_to_operand_aliasing={{0}: (0, {})} | custom-call | tf_op jit(solution)/shard_map/parent_after/pallas_call | solution.py:217
  149.7 0.8 collective-permute-start.20
  150.5 0.7 collective-permute-start.21
  151.3 2.0 collective-permute-start.27
  154.0 0.7 collective-permute-start.24
  154.7 5.8 %collective-permute-done.22.recv_ref = f32[256,256]{1,0:T(8,128)S(1)} collective-permute-done((f32[256,256]{1,0:T(8,128)S(1)}, f32[256,256]{1,0:T(8,128)S(1)}, u32[]{:S(2)}, u32[]{:S(2)}) %collective-permute-start.22) | collective-permute-done | bytes 262176 | tf_op jit(solution)/shard_map/ppermute | solution.py:283
  160.5 0.7 collective-permute-start.25
  161.2 0.9 shard_map.160
  162.1 6.0 %collective-permute-start.26 = (f32[256,256]{1,0:T(8,128)S(1)}, f32[256,256]{1,0:T(8,128)S(1)}, u32[]{:S(2)}, u32[]{:S(2)}) collective-permute-start(f32[256,256]{1,0:T(8,128)S(1)} %get-tuple-element.77.send_ref), channel_id=1, source_target_pairs={{0,2},{1,3},{2,0},{3,1},{4,6},{5,7},{6,4},{7,5},{8,10},{9,11},{10,... | collective-permute-start | bytes 786440 | tf_op jit(solution)/shard_map/ppermute | solution.py:283
  168.1 1.3 shard_map.161
  169.5 0.9 shard_map.162
  170.4 2.6 %collective-permute-start.30 = (f32[256,256]{1,0:T(8,128)S(1)}, f32[256,256]{1,0:T(8,128)S(1)}, u32[]{:S(2)}, u32[]{:S(2)}) collective-permute-start(f32[256,256]{1,0:T(8,128)S(1)} %get-tuple-element.83.send_ref), channel_id=1, source_target_pairs={{0,2},{1,3},{2,0},{3,1},{4,6},{5,7},{6,4},{7,5},{8,10},{9,11},{10,... | collective-permute-start | bytes 786440 | tf_op jit(solution)/shard_map/ppermute | solution.py:283
  173.0 2.3 %collective-permute-done.26.recv_ref = f32[256,256]{1,0:T(8,128)S(1)} collective-permute-done((f32[256,256]{1,0:T(8,128)S(1)}, f32[256,256]{1,0:T(8,128)S(1)}, u32[]{:S(2)}, u32[]{:S(2)}) %collective-permute-start.26) | collective-permute-done | bytes 262176 | tf_op jit(solution)/shard_map/ppermute | solution.py:283
  175.3 1.1 shard_map.163
  176.5 3.0 %collective-permute-start.29 = (f32[256,256]{1,0:T(8,128)S(1)}, f32[256,256]{1,0:T(8,128)S(1)}, u32[]{:S(2)}, u32[]{:S(2)}) collective-permute-start(f32[256,256]{1,0:T(8,128)S(1)} %get-tuple-element.82.send_ref), channel_id=1, source_target_pairs={{0,4},{1,5},{2,6},{3,7},{4,0},{5,1},{6,2},{7,3},{8,12},{9,13},{10,... | collective-permute-start | bytes 786440 | tf_op jit(solution)/shard_map/ppermute | solution.py:283
  179.4 1.3 shard_map.164
  180.8 0.9 shard_map.165
  181.7 0.7 collective-permute-start.32
  182.4 1.3 collective-permute-start.23
  183.7 1.3 collective-permute-start.28
  185.1 0.9 shard_map.166
  186.0 4.5 %collective-permute-start.31 = (f32[256,256]{1,0:T(8,128)S(1)}, f32[256,256]{1,0:T(8,128)S(1)}, u32[]{:S(2)}, u32[]{:S(2)}) collective-permute-start(f32[256,256]{1,0:T(8,128)S(1)} %get-tuple-element.86.send_ref), channel_id=1, source_target_pairs={{0,8},{1,9},{2,10},{3,11},{4,12},{5,13},{6,14},{7,15},{8,0},{9,1},... | collective-permute-start | bytes 786440 | tf_op jit(solution)/shard_map/ppermute | solution.py:283
  190.9 0.9 shard_map.167
  191.9 4.3 %collective-permute-start.33 = (f32[256,256]{1,0:T(8,128)S(1)}, f32[256,256]{1,0:T(8,128)S(1)}, u32[]{:S(2)}, u32[]{:S(2)}) collective-permute-start(f32[256,256]{1,0:T(8,128)S(1)} %get-tuple-element.89.send_ref), channel_id=1, source_target_pairs={{0,8},{1,9},{2,10},{3,11},{4,12},{5,13},{6,14},{7,15},{8,0},{9,1},... | collective-permute-start | bytes 786440 | tf_op jit(solution)/shard_map/ppermute | solution.py:283
  196.2 2.3 %collective-permute-done.23.refs_0_ = f32[128,512]{1,0:T(8,128)S(1)} collective-permute-done((f32[128,512]{1,0:T(8,128)S(1)}, f32[128,512]{1,0:T(8,128)S(1)}, u32[]{:S(2)}, u32[]{:S(2)}) %collective-permute-start.23) | collective-permute-done | bytes 262176 | tf_op jit(solution)/shard_map/ppermute | solution.py:585
  198.5 5.6 %collective-permute-done.28.refs_1_ = f32[128,512]{1,0:T(8,128)S(1)} collective-permute-done((f32[128,512]{1,0:T(8,128)S(1)}, f32[128,512]{1,0:T(8,128)S(1)}, u32[]{:S(2)}, u32[]{:S(2)}) %collective-permute-start.28) | collective-permute-done | bytes 262176 | tf_op jit(solution)/shard_map/ppermute | solution.py:585
  204.1 1.3 fill_roots.1
  205.5 4.3 %collective-permute-done.31.recv_ref = f32[256,256]{1,0:T(8,128)S(1)} collective-permute-done((f32[256,256]{1,0:T(8,128)S(1)}, f32[256,256]{1,0:T(8,128)S(1)}, u32[]{:S(2)}, u32[]{:S(2)}) %collective-permute-start.31) | collective-permute-done | bytes 262176 | tf_op jit(solution)/shard_map/ppermute | solution.py:283
  209.7 0.9 shard_map.168.outs_0_.refs_0_
  210.6 3.2 %collective-permute-done.33.recv_ref = f32[256,256]{1,0:T(8,128)S(1)} collective-permute-done((f32[256,256]{1,0:T(8,128)S(1)}, f32[256,256]{1,0:T(8,128)S(1)}, u32[]{:S(2)}, u32[]{:S(2)}) %collective-permute-start.33) | collective-permute-done | bytes 262176 | tf_op jit(solution)/shard_map/ppermute | solution.py:283
  213.8 0.9 shard_map.169.refs_1_
  214.7 1.4 fill_tops.1
  (83 shorter events, 9.0 us)
Async XLA Ops:
  1.4 5.3 %copy-start.11 = (s32[4]{0:T(128)}, s32[4]{0:T(128)S(1)}, u32[]{:S(2)}) copy-start(s32[4]{0:T(128)S(1)} %pad_add_fusion.info) | copy-start | bytes 52
  1.4 1.0 copy-start
  2.5 1.0 copy-start.2
  4.1 1.4 collective-permute-start
  4.8 0.7 collective-permute-start.1
  6.0 0.7 copy-start.14
  12.3 10.7 %copy-start.19 = (s32[8]{0:T(128)S(1)}, s32[8]{0:T(128)}, u32[]{:S(2)}) copy-start(s32[8]{0:T(128)} %param.21) | copy-start | bytes 100
  12.3 10.7 %copy-start.20 = (s32[16,1]{0,1:T(1,128)S(1)}, s32[16,1]{0,1:T(1,128)}, u32[]{:S(2)}) copy-start(s32[16,1]{0,1:T(1,128)} %param.20) | copy-start | bytes 196
  12.3 10.7 %copy-start.15 = (f32[2,128,256]{2,1,0:T(8,128)S(1)}, f32[2,128,256]{2,1,0:T(8,128)}, u32[]{:S(2)}) copy-start(f32[2,128,256]{2,1,0:T(8,128)} %copy-done.14) | copy-start | bytes 786436
  12.3 12.1 %copy-start.18 = (s32[16,128]{1,0:T(8,128)S(1)}, s32[16,128]{1,0:T(8,128)}, u32[]{:S(2)}) copy-start(s32[16,128]{1,0:T(8,128)} %param.22) | copy-start | bytes 24580
  12.3 12.3 %copy-start.1 = (f32[2,1,256,256]{3,2,1,0:T(8,128)S(1)}, f32[2,1,256,256]{3,2,1,0:T(8,128)}, u32[]{:S(2)}) copy-start(f32[2,1,256,256]{3,2,1,0:T(8,128)} %param.17) | copy-start | bytes 1572868
  12.4 12.3 %copy-start.3 = (f32[2,1,256,256]{3,2,1,0:T(8,128)S(1)}, f32[2,1,256,256]{3,2,1,0:T(8,128)}, u32[]{:S(2)}) copy-start(f32[2,1,256,256]{3,2,1,0:T(8,128)} %param.18) | copy-start | bytes 1572868
  12.4 12.3 %copy-start.12 = (s32[4]{0:T(128)S(1)}, s32[4]{0:T(128)}, u32[]{:S(2)}) copy-start(s32[4]{0:T(128)} %copy-done.11) | copy-start | bytes 52
  18.1 18.1 %copy-start.13 = (s32[4]{0:T(128)S(1)}, s32[4]{0:T(128)}, u32[]{:S(2)}) copy-start(s32[4]{0:T(128)} %copy-done.11) | copy-start | bytes 52
  18.1 18.1 %collective-permute-start.2 = (f32[256,512]{1,0:T(8,128)}, f32[256,512]{1,0:T(8,128)S(1)}, u32[]{:S(2)}, u32[]{:S(2)}) collective-permute-start(f32[256,512]{1,0:T(8,128)} %get-tuple-element.51), channel_id=1, source_target_pairs={{0,1},{2,3},{4,5},{6,7},{8,9},{10,11},{12,13},{14,15},{16,17},{18,... | collective-permute-start | bytes 1572872 | tf_op jit(solution)/shard_map/ppermute | solution.py:365
  21.6 21.3 %collective-permute-start.5 = (f32[256,512]{1,0:T(8,128)}, f32[256,512]{1,0:T(8,128)S(1)}, u32[]{:S(2)}, u32[]{:S(2)}) collective-permute-start(f32[256,512]{1,0:T(8,128)} %get-tuple-element.53.refs_4_), channel_id=1, source_target_pairs={{0,1},{2,3},{4,5},{6,7},{8,9},{10,11},{12,13},{14,15},{16,17},{18,... | collective-permute-start | bytes 1572872 | tf_op jit(solution)/shard_map/ppermute | solution.py:365
  23.1 1.6 collective-permute-start.3
  23.7 0.9 collective-permute-start.4
  24.7 1.0 copy-start.10
  26.3 1.3 copy-start.16
  26.3 11.6 %copy-start.17 = (f32[2,128,256]{2,1,0:T(8,128)}, f32[2,128,256]{2,1,0:T(8,128)S(1)}, u32[]{:S(2)}) copy-start(f32[2,128,256]{2,1,0:T(8,128)S(1)} %get-tuple-element.59) | copy-start | bytes 786436
  26.3 18.8 %collective-permute-start.8 = (f32[2,128,256]{2,1,0:T(8,128)S(1)}, f32[2,128,256]{2,1,0:T(8,128)S(1)}, u32[]{:S(2)}, u32[]{:S(2)}) collective-permute-start(f32[2,128,256]{2,1,0:T(8,128)S(1)} %get-tuple-element.54.rest_0_), channel_id=1, source_target_pairs={{2,1},{6,5},{10,9},{14,13},{18,17},{22,21},{26,25},{30,29},{34,33}... | collective-permute-start | bytes 786440 | tf_op jit(solution)/shard_map/ppermute | solution.py:601
  36.2 1.0 copy-start.7
  37.9 8.7 %copy-start.6 = (f32[1,1,256,256]{3,2,1,0:T(8,128)S(1)}, f32[1,1,256,256]{3,2,1,0:T(8,128)}, u32[]{:S(2)}) copy-start(f32[1,1,256,256]{3,2,1,0:T(8,128)} %param.27) | copy-start | bytes 786436
  37.9 61.7 %collective-permute-start.6 = (f32[256,512]{1,0:T(8,128)S(1)}, f32[256,512]{1,0:T(8,128)S(1)}, u32[]{:S(2)}, u32[]{:S(2)}) collective-permute-start(f32[256,512]{1,0:T(8,128)S(1)} %get-tuple-element.57.refs_0_), channel_id=1, source_target_pairs={{1,2},{5,6},{9,10},{13,14},{17,18},{21,22},{25,26},{29,30},{33,34}... | collective-permute-start | bytes 1572872 | tf_op jit(solution)/shard_map/ppermute | solution.py:369
  38.7 60.8 %collective-permute-start.7 = (f32[256,512]{1,0:T(8,128)S(1)}, f32[256,512]{1,0:T(8,128)S(1)}, u32[]{:S(2)}, u32[]{:S(2)}) collective-permute-start(f32[256,512]{1,0:T(8,128)S(1)} %get-tuple-element.57.refs_0_), channel_id=1, source_target_pairs={{3,2},{7,6},{11,10},{15,14},{19,18},{23,22},{27,26},{31,30},{35,34... | collective-permute-start | bytes 1572872 | tf_op jit(solution)/shard_map/ppermute | solution.py:370
  39.6 6.9 %collective-permute-start.9 = (f32[2,128,256]{2,1,0:T(8,128)}, f32[2,128,256]{2,1,0:T(8,128)S(1)}, u32[]{:S(2)}, u32[]{:S(2)}) collective-permute-start(f32[2,128,256]{2,1,0:T(8,128)} %copy-done.17), channel_id=1, source_target_pairs={{2,3},{6,7},{10,11},{14,15},{18,19},{22,23},{26,27},{30,31},{34,35... | collective-permute-start | bytes 786440 | tf_op jit(solution)/shard_map/ppermute | solution.py:601
  43.6 61.0 %collective-permute-start.10 = (f32[256,512]{1,0:T(8,128)}, f32[256,512]{1,0:T(8,128)}, u32[]{:S(2)}, u32[]{:S(2)}) collective-permute-start(f32[256,512]{1,0:T(8,128)} %get-tuple-element.60.refs_1_), channel_id=1, source_target_pairs={{1,2},{5,6},{9,10},{13,14},{17,18},{21,22},{25,26},{29,30},{33,34}... | collective-permute-start | bytes 1572872 | tf_op jit(solution)/shard_map/ppermute | solution.py:369
  45.0 60.8 %collective-permute-start.11 = (f32[256,512]{1,0:T(8,128)}, f32[256,512]{1,0:T(8,128)}, u32[]{:S(2)}, u32[]{:S(2)}) collective-permute-start(f32[256,512]{1,0:T(8,128)} %get-tuple-element.60.refs_1_), channel_id=1, source_target_pairs={{3,2},{7,6},{11,10},{15,14},{19,18},{23,22},{27,26},{31,30},{35,34... | collective-permute-start | bytes 1572872 | tf_op jit(solution)/shard_map/ppermute | solution.py:370
  46.5 56.7 %collective-permute-start.14 = (f32[1,256,256]{2,1,0:T(8,128)S(1)}, f32[1,256,256]{2,1,0:T(8,128)S(1)}, u32[]{:S(2)}, u32[]{:S(2)}) collective-permute-start(f32[1,256,256]{2,1,0:T(8,128)S(1)} %bitcast.39), channel_id=1, source_target_pairs={{1,0},{3,2},{5,4},{7,6},{9,8},{11,10},{13,12},{15,14},{17,16},{19,... | collective-permute-start | bytes 786440 | tf_op jit(solution)/shard_map/ppermute | solution.py:288
  50.3 76.8 %all-to-all-start = ((f32[16,2,8,512]{3,2,1,0:T(8,128)}), f32[16,2,8,512]{3,2,1,0:T(8,128)}, u32[]{:S(2)}, u32[]{:S(2)}) async-start(f32[16,2,8,512]{3,2,1,0:T(8,128)} %map_rows.1.refs_1_), calls=%async_computation | async-start | bytes 1048576 | tf_op jit(solution)/shard_map/all_to_all | solution.py:563
  100.2 44.8 %copy-start.8 = (f32[1024,128]{1,0:T(8,128)S(1)}, f32[1024,128]{1,0:T(8,128)}, u32[]{:S(2)}) copy-start(f32[1024,128]{1,0:T(8,128)} %get-tuple-element.55.refs_0_.unit_ref) | copy-start | bytes 1572868
  100.2 44.8 %copy-start.9 = (f32[256,640]{1,0:T(8,128)S(1)}, f32[256,640]{1,0:T(8,128)}, u32[]{:S(2)}) copy-start(f32[256,640]{1,0:T(8,128)} %get-tuple-element.65.send_ref) | copy-start | bytes 1966084
  100.2 48.8 %collective-permute-start.12 = (f32[256,512]{1,0:T(8,128)}, f32[256,512]{1,0:T(8,128)}, u32[]{:S(2)}, u32[]{:S(2)}) collective-permute-start(f32[256,512]{1,0:T(8,128)} %get-tuple-element.63), channel_id=1, source_target_pairs={{2,4},{10,12},{18,20},{26,28},{34,36},{42,44},{50,52},{58,60},{66,... | collective-permute-start | bytes 1572872 | tf_op jit(solution)/shard_map/ppermute | solution.py:369
  101.8 47.2 %collective-permute-start.13 = (f32[256,512]{1,0:T(8,128)}, f32[256,512]{1,0:T(8,128)}, u32[]{:S(2)}, u32[]{:S(2)}) collective-permute-start(f32[256,512]{1,0:T(8,128)} %get-tuple-element.63), channel_id=1, source_target_pairs={{6,4},{14,12},{22,20},{30,28},{38,36},{46,44},{54,52},{62,60},{70,... | collective-permute-start | bytes 1572872 | tf_op jit(solution)/shard_map/ppermute | solution.py:370
  103.3 20.8 %collective-permute-start.15 = (f32[1,256,256]{2,1,0:T(8,128)S(1)}, f32[1,256,256]{2,1,0:T(8,128)S(1)}, u32[]{:S(2)}, u32[]{:S(2)}) collective-permute-start(f32[1,256,256]{2,1,0:T(8,128)S(1)} %bitcast.40), channel_id=1, source_target_pairs={{2,0},{6,4},{10,8},{14,12},{18,16},{22,20},{26,24},{30,28},{34,32}... | collective-permute-start | bytes 786440 | tf_op jit(solution)/shard_map/ppermute | solution.py:288
  104.6 21.0 %collective-permute-start.16 = (f32[1,256,256]{2,1,0:T(8,128)S(1)}, f32[1,256,256]{2,1,0:T(8,128)S(1)}, u32[]{:S(2)}, u32[]{:S(2)}) collective-permute-start(f32[1,256,256]{2,1,0:T(8,128)S(1)} %bitcast.41), channel_id=1, source_target_pairs={{4,0},{12,8},{20,16},{28,24},{36,32},{44,40},{52,48},{60,56},{68,6... | collective-permute-start | bytes 786440 | tf_op jit(solution)/shard_map/ppermute | solution.py:288
  105.9 39.1 %collective-permute-start.17 = (f32[1,256,256]{2,1,0:T(8,128)S(1)}, f32[1,256,256]{2,1,0:T(8,128)S(1)}, u32[]{:S(2)}, u32[]{:S(2)}) collective-permute-start(f32[1,256,256]{2,1,0:T(8,128)S(1)} %bitcast.42), channel_id=1, source_target_pairs={{8,0},{24,16},{40,32},{56,48},{72,64},{88,80},{104,96},{120,112}} | collective-permute-start | bytes 786440 | tf_op jit(solution)/shard_map/ppermute | solution.py:288
  124.1 27.2 %collective-permute-start.18 = (f32[256,512]{1,0:T(8,128)}, f32[256,512]{1,0:T(8,128)}, u32[]{:S(2)}, u32[]{:S(2)}) collective-permute-start(f32[256,512]{1,0:T(8,128)} %get-tuple-element.68), channel_id=1, source_target_pairs={{2,4},{10,12},{18,20},{26,28},{34,36},{42,44},{50,52},{58,60},{66,... | collective-permute-start | bytes 1572872 | tf_op jit(solution)/shard_map/ppermute | solution.py:369
  125.6 27.8 %collective-permute-start.19 = (f32[256,512]{1,0:T(8,128)}, f32[256,512]{1,0:T(8,128)}, u32[]{:S(2)}, u32[]{:S(2)}) collective-permute-start(f32[256,512]{1,0:T(8,128)} %get-tuple-element.68), channel_id=1, source_target_pairs={{6,4},{14,12},{22,20},{30,28},{38,36},{46,44},{54,52},{62,60},{70,... | collective-permute-start | bytes 1572872 | tf_op jit(solution)/shard_map/ppermute | solution.py:370
  149.7 11.5 %copy-start.4 = (f32[1,1024,512]{2,1,0:T(8,128)S(1)}, f32[1,1024,512]{2,1,0:T(8,128)}, u32[]{:S(2)}) copy-start(f32[1,1024,512]{2,1,0:T(8,128)} %get-tuple-element.71.top_ref.refs_2_) | copy-start | bytes 6291460
  149.7 11.5 %copy-start.5 = (f32[1,1,256,256]{3,2,1,0:T(8,128)S(1)}, f32[1,1,256,256]{3,2,1,0:T(8,128)}, u32[]{:S(2)}) copy-start(f32[1,1,256,256]{3,2,1,0:T(8,128)} %param.26) | copy-start | bytes 786436
  149.7 12.4 %collective-permute-start.20 = (f32[256,512]{1,0:T(8,128)S(1)}, f32[256,512]{1,0:T(8,128)S(1)}, u32[]{:S(2)}, u32[]{:S(2)}) collective-permute-start(f32[256,512]{1,0:T(8,128)S(1)} %get-tuple-element.69.refs_1_), channel_id=1, source_target_pairs={{4,8},{20,24},{36,40},{52,56},{68,72},{84,88},{100,104},{116,120}} | collective-permute-start | bytes 1572872 | tf_op jit(solution)/shard_map/ppermute | solution.py:369
  150.5 17.6 %collective-permute-start.21 = (f32[256,512]{1,0:T(8,128)S(1)}, f32[256,512]{1,0:T(8,128)S(1)}, u32[]{:S(2)}, u32[]{:S(2)}) collective-permute-start(f32[256,512]{1,0:T(8,128)S(1)} %get-tuple-element.69.refs_1_), channel_id=1, source_target_pairs={{12,8},{28,24},{44,40},{60,56},{76,72},{92,88},{108,104},{124,120}} | collective-permute-start | bytes 1572872 | tf_op jit(solution)/shard_map/ppermute | solution.py:370
  151.2 9.3 %collective-permute-start.22 = (f32[256,256]{1,0:T(8,128)S(1)}, f32[256,256]{1,0:T(8,128)S(1)}, u32[]{:S(2)}, u32[]{:S(2)}) collective-permute-start(f32[256,256]{1,0:T(8,128)S(1)} %get-tuple-element.72.send_ref), channel_id=1, source_target_pairs={{0,1},{1,0},{2,3},{3,2},{4,5},{5,4},{6,7},{7,6},{8,9},{9,8},{10,11... | collective-permute-start | bytes 786440 | tf_op jit(solution)/shard_map/ppermute | solution.py:283
  151.3 18.1 %collective-permute-start.27 = (f32[256,256]{1,0:T(8,128)S(1)}, f32[256,256]{1,0:T(8,128)S(1)}, u32[]{:S(2)}, u32[]{:S(2)}) collective-permute-start(f32[256,256]{1,0:T(8,128)S(1)} %get-tuple-element.66.refs_1_.send_ref), channel_id=1, source_target_pairs={{0,1},{1,0},{2,3},{3,2},{4,5},{5,4},{6,7},{7,6},{8,9},{9,8},{10,11... | collective-permute-start | bytes 786440 | tf_op jit(solution)/shard_map/ppermute | solution.py:283
  154.0 25.5 %collective-permute-start.24 = (f32[256,512]{1,0:T(8,128)S(1)}, f32[256,512]{1,0:T(8,128)S(1)}, u32[]{:S(2)}, u32[]{:S(2)}) collective-permute-start(f32[256,512]{1,0:T(8,128)S(1)} %get-tuple-element.73.outs_0_), channel_id=1, source_target_pairs={{4,8},{20,24},{36,40},{52,56},{68,72},{84,88},{100,104},{116,120}} | collective-permute-start | bytes 1572872 | tf_op jit(solution)/shard_map/ppermute | solution.py:369
  160.5 18.9 %collective-permute-start.25 = (f32[256,512]{1,0:T(8,128)S(1)}, f32[256,512]{1,0:T(8,128)S(1)}, u32[]{:S(2)}, u32[]{:S(2)}) collective-permute-start(f32[256,512]{1,0:T(8,128)S(1)} %get-tuple-element.73.outs_0_), channel_id=1, source_target_pairs={{12,8},{28,24},{44,40},{60,56},{76,72},{92,88},{108,104},{124,120}} | collective-permute-start | bytes 1572872 | tf_op jit(solution)/shard_map/ppermute | solution.py:370
  162.1 13.2 %collective-permute-start.26 = (f32[256,256]{1,0:T(8,128)S(1)}, f32[256,256]{1,0:T(8,128)S(1)}, u32[]{:S(2)}, u32[]{:S(2)}) collective-permute-start(f32[256,256]{1,0:T(8,128)S(1)} %get-tuple-element.77.send_ref), channel_id=1, source_target_pairs={{0,2},{1,3},{2,0},{3,1},{4,6},{5,7},{6,4},{7,5},{8,10},{9,11},{10,... | collective-permute-start | bytes 786440 | tf_op jit(solution)/shard_map/ppermute | solution.py:283
  170.4 10.4 %collective-permute-start.30 = (f32[256,256]{1,0:T(8,128)S(1)}, f32[256,256]{1,0:T(8,128)S(1)}, u32[]{:S(2)}, u32[]{:S(2)}) collective-permute-start(f32[256,256]{1,0:T(8,128)S(1)} %get-tuple-element.83.send_ref), channel_id=1, source_target_pairs={{0,2},{1,3},{2,0},{3,1},{4,6},{5,7},{6,4},{7,5},{8,10},{9,11},{10,... | collective-permute-start | bytes 786440 | tf_op jit(solution)/shard_map/ppermute | solution.py:283
  176.5 8.6 %collective-permute-start.29 = (f32[256,256]{1,0:T(8,128)S(1)}, f32[256,256]{1,0:T(8,128)S(1)}, u32[]{:S(2)}, u32[]{:S(2)}) collective-permute-start(f32[256,256]{1,0:T(8,128)S(1)} %get-tuple-element.82.send_ref), channel_id=1, source_target_pairs={{0,4},{1,5},{2,6},{3,7},{4,0},{5,1},{6,2},{7,3},{8,12},{9,13},{10,... | collective-permute-start | bytes 786440 | tf_op jit(solution)/shard_map/ppermute | solution.py:283
  181.7 9.3 %collective-permute-start.32 = (f32[256,256]{1,0:T(8,128)S(1)}, f32[256,256]{1,0:T(8,128)S(1)}, u32[]{:S(2)}, u32[]{:S(2)}) collective-permute-start(f32[256,256]{1,0:T(8,128)S(1)} %get-tuple-element.87.send_ref), channel_id=1, source_target_pairs={{0,4},{1,5},{2,6},{3,7},{4,0},{5,1},{6,2},{7,3},{8,12},{9,13},{10,... | collective-permute-start | bytes 786440 | tf_op jit(solution)/shard_map/ppermute | solution.py:283
  182.4 16.1 %collective-permute-start.23 = (f32[128,512]{1,0:T(8,128)S(1)}, f32[128,512]{1,0:T(8,128)S(1)}, u32[]{:S(2)}, u32[]{:S(2)}) collective-permute-start(f32[128,512]{1,0:T(8,128)S(1)} %get-tuple-element.75.outs_0_), channel_id=1, source_target_pairs={{8,0},{24,16},{40,32},{56,48},{72,64},{88,80},{104,96},{120,112}} | collective-permute-start | bytes 786440 | tf_op jit(solution)/shard_map/ppermute | solution.py:585
  183.7 20.4 %collective-permute-start.28 = (f32[128,512]{1,0:T(8,128)S(1)}, f32[128,512]{1,0:T(8,128)S(1)}, u32[]{:S(2)}, u32[]{:S(2)}) collective-permute-start(f32[128,512]{1,0:T(8,128)S(1)} %get-tuple-element.80.outs_0_), channel_id=1, source_target_pairs={{8,0},{24,16},{40,32},{56,48},{72,64},{88,80},{104,96},{120,112}} | collective-permute-start | bytes 786440 | tf_op jit(solution)/shard_map/ppermute | solution.py:585
  186.0 23.7 %collective-permute-start.31 = (f32[256,256]{1,0:T(8,128)S(1)}, f32[256,256]{1,0:T(8,128)S(1)}, u32[]{:S(2)}, u32[]{:S(2)}) collective-permute-start(f32[256,256]{1,0:T(8,128)S(1)} %get-tuple-element.86.send_ref), channel_id=1, source_target_pairs={{0,8},{1,9},{2,10},{3,11},{4,12},{5,13},{6,14},{7,15},{8,0},{9,1},... | collective-permute-start | bytes 786440 | tf_op jit(solution)/shard_map/ppermute | solution.py:283
  191.9 21.9 %collective-permute-start.33 = (f32[256,256]{1,0:T(8,128)S(1)}, f32[256,256]{1,0:T(8,128)S(1)}, u32[]{:S(2)}, u32[]{:S(2)}) collective-permute-start(f32[256,256]{1,0:T(8,128)S(1)} %get-tuple-element.89.send_ref), channel_id=1, source_target_pairs={{0,8},{1,9},{2,10},{3,11},{4,12},{5,13},{6,14},{7,15},{8,0},{9,1},... | collective-permute-start | bytes 786440 | tf_op jit(solution)/shard_map/ppermute | solution.py:283

commit v2 on v1

--- a/solution.py
+++ b/solution.py
@@ -226,29 +226,30 @@
     )(upper, unit, send, portion, *after)
 
 
-def tree_level(info, live_at, level, front, top, top_spec, send, recv, node_vectors, node_factors, lead_factors, after=()):
+def tree_level(info, live_at, level, front, top, top_spec, send, recv, node_vectors, node_factors, lead_factors, after=(), into=None, half=0):
     cols = send.shape[1]
     last = level == LEVELS - 1
+    extra = [*after] if into is None else [*after, into]
 
     def kernel(info, top_ref, send_ref, recv_ref, v_ref, g_ref, gl_ref, *outs):
-        out_ref, *outs = outs[len(after) :]
+        out_ref, *outs = outs[len(extra) :]
         lead, rest = role(info, live_at, level)
         top = top_ref[...].reshape(K, cols)
 
         @pl.when(lead)
         def _():
             inner = send_ref[...] + recv_ref[...]
-            out_ref[...] = top - dot3(split(gl_ref[0].T), split(inner), NN)
+            out_ref[...] = (top - dot3(split(gl_ref[0].T), split(inner), NN)).reshape(out_ref.shape)
 
         @pl.when(rest)
         def _():
             inner = send_ref[...] + recv_ref[...]
             weight = dot3(split(g_ref[0].T), split(inner), NN)
-            out_ref[...] = top - dot3(split(v_ref[0]), split(weight), NN)
+            out_ref[...] = (top - dot3(split(v_ref[0]), split(weight), NN)).reshape(out_ref.shape)
 
         @pl.when(jnp.logical_not(lead | rest))
         def _():
-            out_ref[...] = top
+            out_ref[...] = top.reshape(out_ref.shape)
 
         if not last:
             at = info[0] % (4 << level)
@@ -270,12 +271,13 @@
         grid_spec=pltpu.PrefetchScalarGridSpec(
             num_scalar_prefetch=1,
             grid=(1,),
-            in_specs=[top_spec, flat, flat, node, node, node] + [HBM] * len(after),
-            out_specs=[flat] * count,
+            in_specs=[top_spec, flat, flat, node, node, node] + [HBM] * len(extra),
+            out_specs=[flat] * count if into is None else [spec((1, K, cols), (0, 0, half))],
         ),
-        out_shape=[shape] * count,
+        out_shape=[shape] * count if into is None else [jax.ShapeDtypeStruct(into.shape, F32)],
+        input_output_aliases={} if into is None else {6 + len(extra): 0},
         compiler_params=params(),
-    )(info, top, send, recv, node_vectors, node_factors, lead_factors, *after)
+    )(info, top, send, recv, node_vectors, node_factors, lead_factors, *extra)
     return outs
 
 
@@ -399,34 +401,6 @@
         compiler_params=params(),
         name="fill_roots",
     )(info, *leads, applied)
-
-
-def fill_tops(info, applied, front, tops, clear):
-    half = N // len(tops)
-
-    def kernel(info, *refs):
-        out_ref = refs[-1]
-        for i in range(len(tops)):
-            out_ref[0, :, i * half : (i + 1) * half] = refs[i][...]
-        if clear:
-
-            @pl.when(info[0] == 0)
-            def _():
-                out_ref[0, NPIV:, :] = jnp.zeros((K - NPIV, N), F32)
-
-    return pl.pallas_call(
-        kernel,
-        grid_spec=pltpu.PrefetchScalarGridSpec(
-            num_scalar_prefetch=1,
-            grid=(1,),
-            in_specs=[full((K, half))] * len(tops) + [HBM],
-            out_specs=spec((1, K, N), (front, 0, 0)),
-        ),
-        out_shape=jax.ShapeDtypeStruct(applied.shape, F32),
-        input_output_aliases={len(tops) + 1: 0},
-        compiler_params=params(),
-        name="fill_tops",
-    )(info, *tops, applied)
 
 
 def map_node(info, level, lead_in, rest_in, node_vectors, node_factors, after=()):
@@ -586,13 +560,16 @@
             c = chunks[j]
             outs = tree_level(
                 info, 3, level, 0, c[0], c[1], c[2], recvs[j], summit_vectors, summit_factors, lead_factors[level], [order],
+                upper if level == LEVELS - 1 else None, j,
             )
+            if level == LEVELS - 1:
+                upper = outs[0]
             order = outs[0]
             c[0], c[1] = outs[0], full((K, half))
             if level < LEVELS - 1:
                 c[2] = outs[1]
     in_a, in_b = ins["a"], ins["b"]
-    upper_result = fill_tops(info, upper, 0, [c[0] for c in chunks], False)
+    upper_result = upper
     lower_result = fill_roots(info, applied, [in_a, in_b])
     return (lower_result, upper_result)
 

time: 219 us -> 223 us (1.018)
  local copies, waits for them, and re-layouts: 6.35 us -> 13.1 us
  waiting for transfers between devices: 43 us -> 40.2 us
    unnamed x42 -> x55, local copies, waits for them, and re-layouts: 4.94 us -> 11.7 us
    pallas_call x8, Pallas kernels: 7.53 us -> 12 us  [tree_level(): pl.pallas_call(kernel, grid_spec=pltpu.PrefetchScalarGridSpec(num_scalar_...]
    ppermute x8, waiting for transfers between devices: 16.1 us -> 13.1 us  [exchange(): return lax.ppermute(value, 'rows', [(i, i ^ 1 << level) for i in range(16)])]
    pallas_call x1, Pallas kernels: 4.08 us -> 1.29 us  [parent_after(): pl.pallas_call(kernel, grid=(1,), in_specs=[full(upper.shape), full(unit....]
  transfers between devices with their start and end apart: 35 -> 35, of which waited for: 10 -> 9; matrix products, arithmetic and copies ran while one was open for 0% -> 1% of each run, Pallas kernels for 15% -> 14%
where the time goes in v2:
time: 223 us; the launch traced here: 220 us
  starting transfers between devices  103 us (46%)
  Pallas kernels  46.6 us (21%)
  waiting for transfers between devices  40.2 us (18%)
  blocking collectives  16.2 us (7%)
  local copies, waits for them, and re-layouts  13.1 us (6%)
    all_to_all x1, starting transfers between devices, per_device(): swapped = lax.all_to_all(pieces, 'rows', 0, 0)  50.1 us
    ppermute x8, starting transfers between devices, exchange(): return lax.ppermute(value, 'rows', [(i, i ^ 1 << level) for i in range(16)])  22.4 us
    ppermute x4, waiting for transfers between devices, lead_gets(): lax.ppermute(value, 'rows', [(b + step, b) for b in range(0, 16, 2 * step)])  16.3 us
    all_gather x1, blocking collectives, per_device(): portion = lax.all_gather(mine, 'fronts', axis=0, tiled=True)  16.2 us
    ppermute x8, waiting for transfers between devices, exchange(): return lax.ppermute(value, 'rows', [(i, i ^ 1 << level) for i in range(16)])  13.1 us
    pallas_call x8, Pallas kernels, tree_level(): pl.pallas_call(kernel, grid_spec=pltpu.PrefetchScalarGridSpec(num_scalar_...  12 us
    unnamed x55, local copies, waits for them, and re-layouts  11.7 us
    pallas_call x2, Pallas kernels, block_step(): pl.pallas_call(kernel, grid_spec=pltpu.PrefetchScalarGridSpec(num_scalar_...  11.2 us
  transfers between devices with their start and end apart: 35, of which 9 were waited for; matrix products, arithmetic and copies ran while one was open for 1% of the time, Pallas kernels for 14%

profile of v2, /device:TPU:0, one launch (start us, length us, event | category | flops | bytes accessed | tf_op | source)
XLA Modules:
  0.0 220.2 jit_solution(13418397768533613007)
XLA Ops:
  0.6 0.7 dynamic_slice.6
  1.5 1.0 copy-done.1
  2.5 1.0 copy-done.3
  6.8 5.5 %shard_map.151 = (f32[2,1024,512]{2,1,0:T(8,128)}, f32[256,512]{1,0:T(8,128)}) custom-call(s32[4]{0:T(128)} %copy-done.17, f32[2,1024,512]{2,1,0:T(8,128)} %x_hbm.4, f32[2,1024,256]{2,1,0:T(8,128)} %y_hbm.4, f32[2,256,256]{2,1,0:T(8,128)} %bitcast.51, f32[2,128,256]{2,1,0:T(8,128)} %copy-done.20), custom_call_target="tpu_custom_call" | custom-call | tf_op jit(solution)/shard_map/pallas_call | solution.py:112
  12.4 5.7 %shard_map.152 = (f32[2,1024,512]{2,1,0:T(8,128)}, f32[256,512]{1,0:T(8,128)}) custom-call(s32[4]{0:T(128)} %copy-done.17, f32[2,1024,512]{2,1,0:T(8,128)} %x_hbm.4, f32[2,1024,256]{2,1,0:T(8,128)} %y_hbm.4, f32[2,256,256]{2,1,0:T(8,128)} %bitcast.52, f32[2,1024,512]{2,1,0:T(8,128)} %get-tuple-element.49.rest_0_), custom_call_target="tpu_custom_call", output_to_operand_aliasing={{0}: (4, {})} | custom-call | tf_op jit(solution)/shard_map/pallas_call | solution.py:112
  18.1 3.5 %collective-permute-start.2 = (f32[256,512]{1,0:T(8,128)}, f32[256,512]{1,0:T(8,128)S(1)}, u32[]{:S(2)}, u32[]{:S(2)}) collective-permute-start(f32[256,512]{1,0:T(8,128)} %get-tuple-element.51), channel_id=1, source_target_pairs={{0,1},{2,3},{4,5},{6,7},{8,9},{10,11},{12,13},{14,15},{16,17},{18,... | collective-permute-start | bytes 1572872 | tf_op jit(solution)/shard_map/ppermute | solution.py:367
  21.6 1.3 collective-permute-start.5
  24.7 1.0 copy-done.16
  27.6 8.7 %parent_before.1 = (f32[1,1024,512]{2,1,0:T(8,128)}, f32[1024,128]{1,0:T(8,128)}, f32[256,640]{1,0:T(8,128)}) custom-call(s32[4]{0:T(128)} %copy-done.17, f32[1,1024,512]{2,1,0:T(8,128)} %x_hbm.5, f32[1,1024,256]{2,1,0:T(8,128)} %y_hbm.5, f32[1,256,256]{2,1,0:T(8,128)} %bitcast.53, f32[1,256,256]{2,1,0:T(8,128)} %bitcast.30, ...), custom_call_target="tpu_custom_call" | custom-call | tf_op jit(solution)/shard_map/parent_before/pallas_call | solution.py:180
  36.3 1.0 copy-done.13
  37.9 0.8 collective-permute-start.6
  38.8 0.9 collective-permute-start.7
  40.3 2.6 %collective-permute-done.5.lead_ref = f32[256,512]{1,0:T(8,128)S(1)} collective-permute-done((f32[256,512]{1,0:T(8,128)}, f32[256,512]{1,0:T(8,128)S(1)}, u32[]{:S(2)}, u32[]{:S(2)}) %collective-permute-start.5) | collective-permute-done | bytes 524320 | tf_op jit(solution)/shard_map/ppermute | solution.py:367
  43.6 1.5 collective-permute-start.10
  45.0 1.5 collective-permute-start.11
  46.5 1.3 collective-permute-start.14
  47.8 2.4 %map_rows.1.refs_1_ = f32[16,2,8,512]{3,2,1,0:T(8,128)} custom-call(s32[4]{0:T(128)S(1)} %copy-done.19, f32[2,128,256]{2,1,0:T(8,128)S(1)} %collective-permute-done.8.lead_ref, f32[2,128,256]{2,1,0:T(8,128)S(1)} %collective-permute-done.9.rest_ref, f32[256,512]{1,0:T(8,128)S(1)} %get-tuple-element.57.refs_0_, f32[256,512]{1,0:T(8,128)} %get-tuple-element.60.refs_1_), custom_call_target="tpu_custom_call" | custom-call | tf_op jit(solution)/shard_map/map_rows/pallas_call | solution.py:468
  50.2 50.1 %all-to-all-start = ((f32[16,2,8,512]{3,2,1,0:T(8,128)}), f32[16,2,8,512]{3,2,1,0:T(8,128)}, u32[]{:S(2)}, u32[]{:S(2)}) async-start(f32[16,2,8,512]{3,2,1,0:T(8,128)} %map_rows.1.refs_1_), calls=%async_computation | async-start | bytes 1048576 | tf_op jit(solution)/shard_map/all_to_all | solution.py:537
  100.9 1.6 collective-permute-start.12
  102.5 1.4 collective-permute-start.13
  104.0 1.3 collective-permute-start.15
  105.3 1.3 collective-permute-start.16
  106.6 1.3 collective-permute-start.17
  108.5 16.3 %collective-permute-done.15.rest_1_.gl_ref = f32[1,256,256]{2,1,0:T(8,128)S(1)} collective-permute-done((f32[1,256,256]{2,1,0:T(8,128)S(1)}, f32[1,256,256]{2,1,0:T(8,128)S(1)}, u32[]{:S(2)}, u32[]{:S(2)}) %collective-permute-start.15) | collective-permute-done | bytes 262176 | tf_op jit(solution)/shard_map/ppermute | solution.py:290
  124.8 0.7 copy-done.10
  125.5 1.5 collective-permute-start.18
  127.7 1.5 collective-permute-start.19
  129.1 1.7 add_all.1
  130.8 16.2 %all_gather.3.data_ref = f32[16,8,512]{2,1,0:T(8,128)S(1)} all-gather(f32[2,8,512]{2,1,0:T(8,128)} %add_all.1), channel_id=1, replica_groups=mesh['fronts'=8,'rows'=16] {'fronts'}, dimensions={0}, use_global_device_ids=true | all-gather | bytes 294912 | tf_op jit(solution)/shard_map/all_gather | solution.py:543
  147.1 0.9 copy-done.8
  148.0 0.9 copy-done.11
  149.0 1.0 copy-done.14
  150.0 1.1 copy-done.15
  151.1 1.3 parent_after.1
  153.0 0.8 collective-permute-start.20
  154.7 2.0 collective-permute-start.27
  157.3 0.7 collective-permute-start.24
  158.0 5.8 %collective-permute-done.22.recv_ref = f32[256,256]{1,0:T(8,128)S(1)} collective-permute-done((f32[256,256]{1,0:T(8,128)S(1)}, f32[256,256]{1,0:T(8,128)S(1)}, u32[]{:S(2)}, u32[]{:S(2)}) %collective-permute-start.22) | collective-permute-done | bytes 262176 | tf_op jit(solution)/shard_map/ppermute | solution.py:285
  164.5 1.9 shard_map.160
  166.4 6.0 %collective-permute-start.26 = (f32[256,256]{1,0:T(8,128)S(1)}, f32[256,256]{1,0:T(8,128)S(1)}, u32[]{:S(2)}, u32[]{:S(2)}) collective-permute-start(f32[256,256]{1,0:T(8,128)S(1)} %get-tuple-element.77.send_ref), channel_id=1, source_target_pairs={{0,2},{1,3},{2,0},{3,1},{4,6},{5,7},{6,4},{7,5},{8,10},{9,11},{10,... | collective-permute-start | bytes 786440 | tf_op jit(solution)/shard_map/ppermute | solution.py:285
  172.4 1.3 shard_map.161
  173.8 1.9 shard_map.162
  175.6 1.7 collective-permute-start.29
  177.3 1.0 collective-permute-done.26.recv_ref
  178.3 1.1 shard_map.163
  179.5 2.5 %collective-permute-start.31 = (f32[256,256]{1,0:T(8,128)S(1)}, f32[256,256]{1,0:T(8,128)S(1)}, u32[]{:S(2)}, u32[]{:S(2)}) collective-permute-start(f32[256,256]{1,0:T(8,128)S(1)} %get-tuple-element.85.send_ref), channel_id=1, source_target_pairs={{0,4},{1,5},{2,6},{3,7},{4,0},{5,1},{6,2},{7,3},{8,12},{9,13},{10,... | collective-permute-start | bytes 786440 | tf_op jit(solution)/shard_map/ppermute | solution.py:285
  182.0 1.3 shard_map.164
  183.3 0.7 collective-permute-done.29.recv_ref
  184.0 0.9 shard_map.165
  184.9 1.2 collective-permute-start.30
  186.2 1.3 collective-permute-start.23
  187.5 1.3 collective-permute-start.28
  188.8 0.9 shard_map.166
  189.7 4.5 %collective-permute-start.33 = (f32[256,256]{1,0:T(8,128)S(1)}, f32[256,256]{1,0:T(8,128)S(1)}, u32[]{:S(2)}, u32[]{:S(2)}) collective-permute-start(f32[256,256]{1,0:T(8,128)S(1)} %get-tuple-element.89.send_ref), channel_id=1, source_target_pairs={{0,8},{1,9},{2,10},{3,11},{4,12},{5,13},{6,14},{7,15},{8,0},{9,1},... | collective-permute-start | bytes 786440 | tf_op jit(solution)/shard_map/ppermute | solution.py:285
  194.2 0.9 shard_map.167
  195.2 4.4 %collective-permute-start.32 = (f32[256,256]{1,0:T(8,128)S(1)}, f32[256,256]{1,0:T(8,128)S(1)}, u32[]{:S(2)}, u32[]{:S(2)}) collective-permute-start(f32[256,256]{1,0:T(8,128)S(1)} %get-tuple-element.88.send_ref), channel_id=1, source_target_pairs={{0,8},{1,9},{2,10},{3,11},{4,12},{5,13},{6,14},{7,15},{8,0},{9,1},... | collective-permute-start | bytes 786440 | tf_op jit(solution)/shard_map/ppermute | solution.py:285
  199.5 2.5 %collective-permute-done.23.refs_0_ = f32[128,512]{1,0:T(8,128)S(1)} collective-permute-done((f32[128,512]{1,0:T(8,128)S(1)}, f32[128,512]{1,0:T(8,128)S(1)}, u32[]{:S(2)}, u32[]{:S(2)}) %collective-permute-start.23) | collective-permute-done | bytes 262176 | tf_op jit(solution)/shard_map/ppermute | solution.py:559
  202.0 5.6 %collective-permute-done.28.refs_1_ = f32[128,512]{1,0:T(8,128)S(1)} collective-permute-done((f32[128,512]{1,0:T(8,128)S(1)}, f32[128,512]{1,0:T(8,128)S(1)}, u32[]{:S(2)}, u32[]{:S(2)}) %collective-permute-start.28) | collective-permute-done | bytes 262176 | tf_op jit(solution)/shard_map/ppermute | solution.py:559
  207.7 1.3 fill_roots.1
  209.0 4.3 %collective-permute-done.33.recv_ref = f32[256,256]{1,0:T(8,128)S(1)} collective-permute-done((f32[256,256]{1,0:T(8,128)S(1)}, f32[256,256]{1,0:T(8,128)S(1)}, u32[]{:S(2)}, u32[]{:S(2)}) %collective-permute-start.33) | collective-permute-done | bytes 262176 | tf_op jit(solution)/shard_map/ppermute | solution.py:285
  213.3 1.9 shard_map.168.outs_0_
  215.1 1.3 copy.41.outs_1_
  216.4 1.2 collective-permute-done.32.recv_ref
  217.7 2.5 %shard_map.169 = f32[1,1024,512]{2,1,0:T(8,128)} custom-call(s32[4]{0:T(128)S(1)} %copy-done.19, f32[256,256]{1,0:T(8,128)S(1)} %get-tuple-element.87.outs_0_.top_ref, f32[256,256]{1,0:T(8,128)S(1)} %get-tuple-element.88.send_ref, f32[256,256]{1,0:T(8,128)S(1)} %collective-permute-done.32.recv_ref, ...), custom_call_target="tpu_custom_call", output_to_operand_aliasing={{}: (8, {})} | custom-call | tf_op jit(solution)/shard_map/pallas_call | solution.py:269
  (95 shorter events, 13.3 us)
Async XLA Ops:
  1.4 5.3 %copy-start.17 = (s32[4]{0:T(128)}, s32[4]{0:T(128)S(1)}, u32[]{:S(2)}) copy-start(s32[4]{0:T(128)S(1)} %pad_add_fusion.info) | copy-start | bytes 52
  1.4 1.0 copy-start.1
  2.5 1.0 copy-start.3
  4.1 1.4 collective-permute-start
  4.8 0.7 collective-permute-start.1
  6.0 0.7 copy-start.20
  12.3 10.7 %copy-start.25 = (s32[8]{0:T(128)S(1)}, s32[8]{0:T(128)}, u32[]{:S(2)}) copy-start(s32[8]{0:T(128)} %param.21) | copy-start | bytes 100
  12.3 10.7 %copy-start.26 = (s32[16,1]{0,1:T(1,128)S(1)}, s32[16,1]{0,1:T(1,128)}, u32[]{:S(2)}) copy-start(s32[16,1]{0,1:T(1,128)} %param.20) | copy-start | bytes 196
  12.3 10.7 %copy-start.21 = (f32[2,128,256]{2,1,0:T(8,128)S(1)}, f32[2,128,256]{2,1,0:T(8,128)}, u32[]{:S(2)}) copy-start(f32[2,128,256]{2,1,0:T(8,128)} %copy-done.20) | copy-start | bytes 786436
  12.3 12.1 %copy-start.24 = (s32[16,128]{1,0:T(8,128)S(1)}, s32[16,128]{1,0:T(8,128)}, u32[]{:S(2)}) copy-start(s32[16,128]{1,0:T(8,128)} %param.22) | copy-start | bytes 24580
  12.3 12.3 %copy-start.2 = (f32[2,1,256,256]{3,2,1,0:T(8,128)S(1)}, f32[2,1,256,256]{3,2,1,0:T(8,128)}, u32[]{:S(2)}) copy-start(f32[2,1,256,256]{3,2,1,0:T(8,128)} %param.17) | copy-start | bytes 1572868
  12.4 12.3 %copy-start.4 = (f32[2,1,256,256]{3,2,1,0:T(8,128)S(1)}, f32[2,1,256,256]{3,2,1,0:T(8,128)}, u32[]{:S(2)}) copy-start(f32[2,1,256,256]{3,2,1,0:T(8,128)} %param.18) | copy-start | bytes 1572868
  12.4 12.3 %copy-start.18 = (s32[4]{0:T(128)S(1)}, s32[4]{0:T(128)}, u32[]{:S(2)}) copy-start(s32[4]{0:T(128)} %copy-done.17) | copy-start | bytes 52
  18.1 18.2 %copy-start.19 = (s32[4]{0:T(128)S(1)}, s32[4]{0:T(128)}, u32[]{:S(2)}) copy-start(s32[4]{0:T(128)} %copy-done.17) | copy-start | bytes 52
  18.1 18.2 %collective-permute-start.2 = (f32[256,512]{1,0:T(8,128)}, f32[256,512]{1,0:T(8,128)S(1)}, u32[]{:S(2)}, u32[]{:S(2)}) collective-permute-start(f32[256,512]{1,0:T(8,128)} %get-tuple-element.51), channel_id=1, source_target_pairs={{0,1},{2,3},{4,5},{6,7},{8,9},{10,11},{12,13},{14,15},{16,17},{18,... | collective-permute-start | bytes 1572872 | tf_op jit(solution)/shard_map/ppermute | solution.py:367
  21.6 21.3 %collective-permute-start.5 = (f32[256,512]{1,0:T(8,128)}, f32[256,512]{1,0:T(8,128)S(1)}, u32[]{:S(2)}, u32[]{:S(2)}) collective-permute-start(f32[256,512]{1,0:T(8,128)} %get-tuple-element.53.refs_4_), channel_id=1, source_target_pairs={{0,1},{2,3},{4,5},{6,7},{8,9},{10,11},{12,13},{14,15},{16,17},{18,... | collective-permute-start | bytes 1572872 | tf_op jit(solution)/shard_map/ppermute | solution.py:367
  23.1 1.6 collective-permute-start.3
  23.7 0.9 collective-permute-start.4
  24.7 1.0 copy-start.16
  26.3 1.3 copy-start.22
  26.3 10.0 %copy-start.23 = (f32[2,128,256]{2,1,0:T(8,128)}, f32[2,128,256]{2,1,0:T(8,128)S(1)}, u32[]{:S(2)}) copy-start(f32[2,128,256]{2,1,0:T(8,128)S(1)} %get-tuple-element.59) | copy-start | bytes 786436
  26.3 18.7 %collective-permute-start.8 = (f32[2,128,256]{2,1,0:T(8,128)S(1)}, f32[2,128,256]{2,1,0:T(8,128)S(1)}, u32[]{:S(2)}, u32[]{:S(2)}) collective-permute-start(f32[2,128,256]{2,1,0:T(8,128)S(1)} %get-tuple-element.54.rest_0_), channel_id=1, source_target_pairs={{2,1},{6,5},{10,9},{14,13},{18,17},{22,21},{26,25},{30,29},{34,33}... | collective-permute-start | bytes 786440 | tf_op jit(solution)/shard_map/ppermute | solution.py:578
  36.3 1.0 copy-start.13
  37.9 8.6 %copy-start.6 = (f32[1,1,256,256]{3,2,1,0:T(8,128)S(1)}, f32[1,1,256,256]{3,2,1,0:T(8,128)}, u32[]{:S(2)}) copy-start(f32[1,1,256,256]{3,2,1,0:T(8,128)} %param.27) | copy-start | bytes 786436
  37.9 62.3 %collective-permute-start.6 = (f32[256,512]{1,0:T(8,128)S(1)}, f32[256,512]{1,0:T(8,128)S(1)}, u32[]{:S(2)}, u32[]{:S(2)}) collective-permute-start(f32[256,512]{1,0:T(8,128)S(1)} %get-tuple-element.57.refs_0_), channel_id=1, source_target_pairs={{1,2},{5,6},{9,10},{13,14},{17,18},{21,22},{25,26},{29,30},{33,34}... | collective-permute-start | bytes 1572872 | tf_op jit(solution)/shard_map/ppermute | solution.py:371
  38.8 61.5 %collective-permute-start.7 = (f32[256,512]{1,0:T(8,128)S(1)}, f32[256,512]{1,0:T(8,128)S(1)}, u32[]{:S(2)}, u32[]{:S(2)}) collective-permute-start(f32[256,512]{1,0:T(8,128)S(1)} %get-tuple-element.57.refs_0_), channel_id=1, source_target_pairs={{3,2},{7,6},{11,10},{15,14},{19,18},{23,22},{27,26},{31,30},{35,34... | collective-permute-start | bytes 1572872 | tf_op jit(solution)/shard_map/ppermute | solution.py:372
  39.7 6.8 %collective-permute-start.9 = (f32[2,128,256]{2,1,0:T(8,128)}, f32[2,128,256]{2,1,0:T(8,128)S(1)}, u32[]{:S(2)}, u32[]{:S(2)}) collective-permute-start(f32[2,128,256]{2,1,0:T(8,128)} %copy-done.23), channel_id=1, source_target_pairs={{2,3},{6,7},{10,11},{14,15},{18,19},{22,23},{26,27},{30,31},{34,35... | collective-permute-start | bytes 786440 | tf_op jit(solution)/shard_map/ppermute | solution.py:578
  43.6 61.7 %collective-permute-start.10 = (f32[256,512]{1,0:T(8,128)}, f32[256,512]{1,0:T(8,128)}, u32[]{:S(2)}, u32[]{:S(2)}) collective-permute-start(f32[256,512]{1,0:T(8,128)} %get-tuple-element.60.refs_1_), channel_id=1, source_target_pairs={{1,2},{5,6},{9,10},{13,14},{17,18},{21,22},{25,26},{29,30},{33,34}... | collective-permute-start | bytes 1572872 | tf_op jit(solution)/shard_map/ppermute | solution.py:371
  45.0 61.6 %collective-permute-start.11 = (f32[256,512]{1,0:T(8,128)}, f32[256,512]{1,0:T(8,128)}, u32[]{:S(2)}, u32[]{:S(2)}) collective-permute-start(f32[256,512]{1,0:T(8,128)} %get-tuple-element.60.refs_1_), channel_id=1, source_target_pairs={{3,2},{7,6},{11,10},{15,14},{19,18},{23,22},{27,26},{31,30},{35,34... | collective-permute-start | bytes 1572872 | tf_op jit(solution)/shard_map/ppermute | solution.py:372
  46.5 57.5 %collective-permute-start.14 = (f32[1,256,256]{2,1,0:T(8,128)S(1)}, f32[1,256,256]{2,1,0:T(8,128)}, u32[]{:S(2)}, u32[]{:S(2)}) collective-permute-start(f32[1,256,256]{2,1,0:T(8,128)S(1)} %bitcast.39), channel_id=1, source_target_pairs={{1,0},{3,2},{5,4},{7,6},{9,8},{11,10},{13,12},{15,14},{17,16},{19,... | collective-permute-start | bytes 786440 | tf_op jit(solution)/shard_map/ppermute | solution.py:290
  50.2 78.9 %all-to-all-start = ((f32[16,2,8,512]{3,2,1,0:T(8,128)}), f32[16,2,8,512]{3,2,1,0:T(8,128)}, u32[]{:S(2)}, u32[]{:S(2)}) async-start(f32[16,2,8,512]{3,2,1,0:T(8,128)} %map_rows.1.refs_1_), calls=%async_computation | async-start | bytes 1048576 | tf_op jit(solution)/shard_map/all_to_all | solution.py:537
  100.9 46.1 %copy-start = (f32[1,1024,512]{2,1,0:T(8,128)S(1)}, f32[1,1024,512]{2,1,0:T(8,128)}, u32[]{:S(2)}) copy-start(f32[1,1024,512]{2,1,0:T(8,128)} %get-tuple-element.64.x_ref) | copy-start | bytes 6291460
  100.9 51.5 %collective-permute-start.12 = (f32[256,512]{1,0:T(8,128)}, f32[256,512]{1,0:T(8,128)}, u32[]{:S(2)}, u32[]{:S(2)}) collective-permute-start(f32[256,512]{1,0:T(8,128)} %get-tuple-element.63), channel_id=1, source_target_pairs={{2,4},{10,12},{18,20},{26,28},{34,36},{42,44},{50,52},{58,60},{66,... | collective-permute-start | bytes 1572872 | tf_op jit(solution)/shard_map/ppermute | solution.py:371
  102.5 49.9 %collective-permute-start.13 = (f32[256,512]{1,0:T(8,128)}, f32[256,512]{1,0:T(8,128)}, u32[]{:S(2)}, u32[]{:S(2)}) collective-permute-start(f32[256,512]{1,0:T(8,128)} %get-tuple-element.63), channel_id=1, source_target_pairs={{6,4},{14,12},{22,20},{30,28},{38,36},{46,44},{54,52},{62,60},{70,... | collective-permute-start | bytes 1572872 | tf_op jit(solution)/shard_map/ppermute | solution.py:372
  104.0 20.8 %collective-permute-start.15 = (f32[1,256,256]{2,1,0:T(8,128)S(1)}, f32[1,256,256]{2,1,0:T(8,128)S(1)}, u32[]{:S(2)}, u32[]{:S(2)}) collective-permute-start(f32[1,256,256]{2,1,0:T(8,128)S(1)} %bitcast.40), channel_id=1, source_target_pairs={{2,0},{6,4},{10,8},{14,12},{18,16},{22,20},{26,24},{30,28},{34,32}... | collective-permute-start | bytes 786440 | tf_op jit(solution)/shard_map/ppermute | solution.py:290
  105.3 21.7 %collective-permute-start.16 = (f32[1,256,256]{2,1,0:T(8,128)S(1)}, f32[1,256,256]{2,1,0:T(8,128)S(1)}, u32[]{:S(2)}, u32[]{:S(2)}) collective-permute-start(f32[1,256,256]{2,1,0:T(8,128)S(1)} %bitcast.41), channel_id=1, source_target_pairs={{4,0},{12,8},{20,16},{28,24},{36,32},{44,40},{52,48},{60,56},{68,6... | collective-permute-start | bytes 786440 | tf_op jit(solution)/shard_map/ppermute | solution.py:290
  106.6 40.5 %collective-permute-start.17 = (f32[1,256,256]{2,1,0:T(8,128)S(1)}, f32[1,256,256]{2,1,0:T(8,128)}, u32[]{:S(2)}, u32[]{:S(2)}) collective-permute-start(f32[1,256,256]{2,1,0:T(8,128)S(1)} %bitcast.42), channel_id=1, source_target_pairs={{8,0},{24,16},{40,32},{56,48},{72,64},{88,80},{104,96},{120,112}} | collective-permute-start | bytes 786440 | tf_op jit(solution)/shard_map/ppermute | solution.py:290
  124.8 0.7 copy-start.10
  125.5 29.1 %collective-permute-start.18 = (f32[256,512]{1,0:T(8,128)}, f32[256,512]{1,0:T(8,128)}, u32[]{:S(2)}, u32[]{:S(2)}) collective-permute-start(f32[256,512]{1,0:T(8,128)} %get-tuple-element.68), channel_id=1, source_target_pairs={{2,4},{10,12},{18,20},{26,28},{34,36},{42,44},{50,52},{58,60},{66,... | collective-permute-start | bytes 1572872 | tf_op jit(solution)/shard_map/ppermute | solution.py:371
  127.0 0.7 copy-start.7
  127.7 29.0 %collective-permute-start.19 = (f32[256,512]{1,0:T(8,128)}, f32[256,512]{1,0:T(8,128)}, u32[]{:S(2)}, u32[]{:S(2)}) collective-permute-start(f32[256,512]{1,0:T(8,128)} %get-tuple-element.68), channel_id=1, source_target_pairs={{6,4},{14,12},{22,20},{30,28},{38,36},{46,44},{54,52},{62,60},{70,... | collective-permute-start | bytes 1572872 | tf_op jit(solution)/shard_map/ppermute | solution.py:372
  147.1 1.0 copy-start.8
  148.0 0.9 copy-start.11
  149.0 1.0 copy-start.14
  150.0 1.1 copy-start.15
  153.0 11.5 %copy-start.5 = (f32[1,1,256,256]{3,2,1,0:T(8,128)S(1)}, f32[1,1,256,256]{3,2,1,0:T(8,128)}, u32[]{:S(2)}) copy-start(f32[1,1,256,256]{3,2,1,0:T(8,128)} %param.26) | copy-start | bytes 786436
  153.0 13.4 %collective-permute-start.20 = (f32[256,512]{1,0:T(8,128)S(1)}, f32[256,512]{1,0:T(8,128)S(1)}, u32[]{:S(2)}, u32[]{:S(2)}) collective-permute-start(f32[256,512]{1,0:T(8,128)S(1)} %get-tuple-element.69.refs_1_), channel_id=1, source_target_pairs={{4,8},{20,24},{36,40},{52,56},{68,72},{84,88},{100,104},{116,120}} | collective-permute-start | bytes 1572872 | tf_op jit(solution)/shard_map/ppermute | solution.py:371
  153.9 18.5 %collective-permute-start.21 = (f32[256,512]{1,0:T(8,128)S(1)}, f32[256,512]{1,0:T(8,128)S(1)}, u32[]{:S(2)}, u32[]{:S(2)}) collective-permute-start(f32[256,512]{1,0:T(8,128)S(1)} %get-tuple-element.69.refs_1_), channel_id=1, source_target_pairs={{12,8},{28,24},{44,40},{60,56},{76,72},{92,88},{108,104},{124,120}} | collective-permute-start | bytes 1572872 | tf_op jit(solution)/shard_map/ppermute | solution.py:372
  154.6 9.3 %collective-permute-start.22 = (f32[256,256]{1,0:T(8,128)S(1)}, f32[256,256]{1,0:T(8,128)S(1)}, u32[]{:S(2)}, u32[]{:S(2)}) collective-permute-start(f32[256,256]{1,0:T(8,128)S(1)} %get-tuple-element.72.send_ref), channel_id=1, source_target_pairs={{0,1},{1,0},{2,3},{3,2},{4,5},{5,4},{6,7},{7,6},{8,9},{9,8},{10,11... | collective-permute-start | bytes 786440 | tf_op jit(solution)/shard_map/ppermute | solution.py:285
  154.7 19.1 %collective-permute-start.27 = (f32[256,256]{1,0:T(8,128)S(1)}, f32[256,256]{1,0:T(8,128)S(1)}, u32[]{:S(2)}, u32[]{:S(2)}) collective-permute-start(f32[256,256]{1,0:T(8,128)S(1)} %get-tuple-element.66.refs_1_.send_ref), channel_id=1, source_target_pairs={{0,1},{1,0},{2,3},{3,2},{4,5},{5,4},{6,7},{7,6},{8,9},{9,8},{10,11... | collective-permute-start | bytes 786440 | tf_op jit(solution)/shard_map/ppermute | solution.py:285
  157.3 24.6 %collective-permute-start.24 = (f32[256,512]{1,0:T(8,128)S(1)}, f32[256,512]{1,0:T(8,128)S(1)}, u32[]{:S(2)}, u32[]{:S(2)}) collective-permute-start(f32[256,512]{1,0:T(8,128)S(1)} %get-tuple-element.73.outs_0_), channel_id=1, source_target_pairs={{4,8},{20,24},{36,40},{52,56},{68,72},{84,88},{100,104},{116,120}} | collective-permute-start | bytes 1572872 | tf_op jit(solution)/shard_map/ppermute | solution.py:371
  163.8 18.1 %collective-permute-start.25 = (f32[256,512]{1,0:T(8,128)S(1)}, f32[256,512]{1,0:T(8,128)S(1)}, u32[]{:S(2)}, u32[]{:S(2)}) collective-permute-start(f32[256,512]{1,0:T(8,128)S(1)} %get-tuple-element.73.outs_0_), channel_id=1, source_target_pairs={{12,8},{28,24},{44,40},{60,56},{76,72},{92,88},{108,104},{124,120}} | collective-permute-start | bytes 1572872 | tf_op jit(solution)/shard_map/ppermute | solution.py:372
  166.4 11.9 %collective-permute-start.26 = (f32[256,256]{1,0:T(8,128)S(1)}, f32[256,256]{1,0:T(8,128)S(1)}, u32[]{:S(2)}, u32[]{:S(2)}) collective-permute-start(f32[256,256]{1,0:T(8,128)S(1)} %get-tuple-element.77.send_ref), channel_id=1, source_target_pairs={{0,2},{1,3},{2,0},{3,1},{4,6},{5,7},{6,4},{7,5},{8,10},{9,11},{10,... | collective-permute-start | bytes 786440 | tf_op jit(solution)/shard_map/ppermute | solution.py:285
  172.4 5.9 %copy-start.12 = (f32[1,256,256]{2,1,0:T(8,128)S(1)}, f32[1,256,256]{2,1,0:T(8,128)}, u32[]{:S(2)}) copy-start(f32[1,256,256]{2,1,0:T(8,128)} %copy-done.10) | copy-start | bytes 786436
  175.6 8.4 %collective-permute-start.29 = (f32[256,256]{1,0:T(8,128)S(1)}, f32[256,256]{1,0:T(8,128)S(1)}, u32[]{:S(2)}, u32[]{:S(2)}) collective-permute-start(f32[256,256]{1,0:T(8,128)S(1)} %get-tuple-element.82.send_ref), channel_id=1, source_target_pairs={{0,2},{1,3},{2,0},{3,1},{4,6},{5,7},{6,4},{7,5},{8,10},{9,11},{10,... | collective-permute-start | bytes 786440 | tf_op jit(solution)/shard_map/ppermute | solution.py:285
  179.5 9.3 %collective-permute-start.31 = (f32[256,256]{1,0:T(8,128)S(1)}, f32[256,256]{1,0:T(8,128)S(1)}, u32[]{:S(2)}, u32[]{:S(2)}) collective-permute-start(f32[256,256]{1,0:T(8,128)S(1)} %get-tuple-element.85.send_ref), channel_id=1, source_target_pairs={{0,4},{1,5},{2,6},{3,7},{4,0},{5,1},{6,2},{7,3},{8,12},{9,13},{10,... | collective-permute-start | bytes 786440 | tf_op jit(solution)/shard_map/ppermute | solution.py:285
  181.9 6.8 %copy-start.9 = (f32[1,256,256]{2,1,0:T(8,128)S(1)}, f32[1,256,256]{2,1,0:T(8,128)}, u32[]{:S(2)}) copy-start(f32[1,256,256]{2,1,0:T(8,128)} %copy-done.7) | copy-start | bytes 786436
  184.9 9.3 %collective-permute-start.30 = (f32[256,256]{1,0:T(8,128)S(1)}, f32[256,256]{1,0:T(8,128)S(1)}, u32[]{:S(2)}, u32[]{:S(2)}) collective-permute-start(f32[256,256]{1,0:T(8,128)S(1)} %get-tuple-element.84.send_ref), channel_id=1, source_target_pairs={{0,4},{1,5},{2,6},{3,7},{4,0},{5,1},{6,2},{7,3},{8,12},{9,13},{10,... | collective-permute-start | bytes 786440 | tf_op jit(solution)/shard_map/ppermute | solution.py:285
  186.2 15.9 %collective-permute-start.23 = (f32[128,512]{1,0:T(8,128)S(1)}, f32[128,512]{1,0:T(8,128)S(1)}, u32[]{:S(2)}, u32[]{:S(2)}) collective-permute-start(f32[128,512]{1,0:T(8,128)S(1)} %get-tuple-element.75.outs_0_), channel_id=1, source_target_pairs={{8,0},{24,16},{40,32},{56,48},{72,64},{88,80},{104,96},{120,112}} | collective-permute-start | bytes 786440 | tf_op jit(solution)/shard_map/ppermute | solution.py:559
  187.5 20.2 %collective-permute-start.28 = (f32[128,512]{1,0:T(8,128)S(1)}, f32[128,512]{1,0:T(8,128)S(1)}, u32[]{:S(2)}, u32[]{:S(2)}) collective-permute-start(f32[128,512]{1,0:T(8,128)S(1)} %get-tuple-element.80.outs_0_), channel_id=1, source_target_pairs={{8,0},{24,16},{40,32},{56,48},{72,64},{88,80},{104,96},{120,112}} | collective-permute-start | bytes 786440 | tf_op jit(solution)/shard_map/ppermute | solution.py:559
  189.7 23.6 %collective-permute-start.33 = (f32[256,256]{1,0:T(8,128)S(1)}, f32[256,256]{1,0:T(8,128)S(1)}, u32[]{:S(2)}, u32[]{:S(2)}) collective-permute-start(f32[256,256]{1,0:T(8,128)S(1)} %get-tuple-element.89.send_ref), channel_id=1, source_target_pairs={{0,8},{1,9},{2,10},{3,11},{4,12},{5,13},{6,14},{7,15},{8,0},{9,1},... | collective-permute-start | bytes 786440 | tf_op jit(solution)/shard_map/ppermute | solution.py:285
  195.2 22.5 %collective-permute-start.32 = (f32[256,256]{1,0:T(8,128)S(1)}, f32[256,256]{1,0:T(8,128)S(1)}, u32[]{:S(2)}, u32[]{:S(2)}) collective-permute-start(f32[256,256]{1,0:T(8,128)S(1)} %get-tuple-element.88.send_ref), channel_id=1, source_target_pairs={{0,8},{1,9},{2,10},{3,11},{4,12},{5,13},{6,14},{7,15},{8,0},{9,1},... | collective-permute-start | bytes 786440 | tf_op jit(solution)/shard_map/ppermute | solution.py:285
